TPU v7x, 128 devices: a whole 4x4x4 slice. The times are simulated.
128 devices in a mesh: grp: 4 (over x), dev: 32 (over z, y, core).
Axes of the slice: x: 4, y: 4, z: 4, core: 2. Of those that a mesh axis runs over, the one named last changes fastest.
Arguments:
- cache_k: bfloat16 [64, 8, 1024, 128], P('grp', None, 'dev')
- cache_v: bfloat16 [64, 8, 1024, 128], P('grp', None, 'dev'), may hold values from -6 to 6
- source: int32 [64], replicated, may hold values from 0 to 63, as said below
- lengths: int32 [64], P('grp'), may hold values from 1 to 1023
- query: bfloat16 [64, 6144], P('grp')
- new_key: bfloat16 [64, 8, 128], P('grp'), may hold values from -6 to 6
- new_value: bfloat16 [64, 8, 128], P('grp'), may hold values from -6 to 6
- resid: bfloat16 [64, 6144], P('grp', 'dev'), may hold values from -6 to 6
- out_weight: bfloat16 [6144, 6144], P('dev'), may hold values from -0.078125 to 0.078125
- norm_gain: bfloat16 [6144], replicated, may hold values from 0.099609375 to 1.8984375
- w_gate: bfloat16 [6144, 65536], P(None, ('grp', 'dev')), may hold values from -0.078125 to 0.078125
- w_up: bfloat16 [6144, 65536], P(None, ('grp', 'dev')), may hold values from -0.078125 to 0.078125
- w_down: bfloat16 [65536, 6144], P(('grp', 'dev')), may hold values from -0.0625 to 0.0625
- expert_ids: int32 [64, 2], P('grp'), may hold values from 0 to 7, all different within a row; in each aligned block of 16 rows (0 to 15, 16 to 31, ...) at most 8 rows name the same one
- gate_codes: int32 [64, 2], P('grp'), may hold values from 1 to 1023
Outputs:
- new_cache_k: bfloat16 [64, 8, 1024, 128], P('grp', None, 'dev')
- new_cache_v: bfloat16 [64, 8, 1024, 128], P('grp', None, 'dev')
- layer_out: bfloat16 [64, 6144], P('grp', 'dev')
Inputs may be any that keep to these rules, and one draw needn't show every extreme that they name: source is a permutation of the 64 slots; each group of 16 slots sends exactly 2 of its requests to each other group and receives exactly 2 from each other group into the slots it vacated; every other slot keeps its own request. `expert_ids`: in the 16 rows of each group no expert is named more than 8 times.
All inputs are finite; a program needn't handle non-finite values.
Results may differ from a plain program's by a relative error of at most 0.012.
Values may be sent and summed in bfloat16 or wider, within the bound.
No kernel may reach another device: no remote copies, remote signals or barrier semaphores. Data moves between devices by JAX's collectives and lax.ppermute only.
A program may use at most 128 MiB of HBM per device.

v0:
```python
import jax
import jax.numpy as jnp
from jax import lax
from jax.sharding import PartitionSpec as P

EXPERTS = 8
TOP = 2
MOVE = 2
CAP = 8


def expert_ffn(rows, w_gate, w_up, w_down):
    gate_val = jnp.dot(rows, w_gate, preferred_element_type=jnp.float32)
    up_val = jnp.dot(rows, w_up, preferred_element_type=jnp.float32)
    hidden = (jax.nn.silu(gate_val) * up_val).astype(jnp.bfloat16)
    return jnp.dot(hidden, w_down, preferred_element_type=jnp.float32)


def on_device(
    cache_k,
    cache_v,
    source,
    lengths,
    query,
    new_key,
    new_value,
    resid,
    out_weight,
    norm_gain,
    w_gate,
    w_up,
    w_down,
    expert_ids,
    gate_codes,
):
    group_count = lax.axis_size("grp")
    dev_count = lax.axis_size("dev")
    group_id = lax.axis_index("grp")
    dev_id = lax.axis_index("dev")
    per_group, kv_heads, block_len, head_dim = cache_k.shape
    all_slots = source.shape[0]
    model_width = resid.shape[1] * dev_count
    feat_width = resid.shape[1]
    slot_range = jnp.arange(all_slots, dtype=jnp.int32)
    inverse = jnp.sum(
        jnp.where(source[:, None] == slot_range[None, :], slot_range[:, None], 0), axis=0
    )
    old_group = slot_range // per_group
    dest_group = inverse // per_group
    leaving = dest_group != old_group
    same_route = (old_group[:, None] == old_group[None, :]) & (
        dest_group[:, None] == dest_group[None, :]
    )
    earlier_movers = same_route & leaving[None, :] & (slot_range[None, :] < slot_range[:, None])
    mover_rank = jnp.sum(earlier_movers.astype(jnp.int32), axis=1)
    first_slot = group_id * per_group
    my_leaving = lax.dynamic_slice_in_dim(leaving, first_slot, per_group)
    my_dest = lax.dynamic_slice_in_dim(dest_group, first_slot, per_group)
    my_rank = lax.dynamic_slice_in_dim(mover_rank, first_slot, per_group)
    buffer_range = jnp.arange(group_count * MOVE, dtype=jnp.int32)
    local_range = jnp.arange(per_group, dtype=jnp.int32)
    match = (
        my_leaving[None, :]
        & (my_dest[None, :] == (buffer_range // MOVE)[:, None])
        & (my_rank[None, :] == (buffer_range % MOVE)[:, None])
    )
    picked = jnp.sum(jnp.where(match, local_range[None, :], 0), axis=1)
    filled = jnp.any(match, axis=1)[:, None, None, None]
    zero_block = jnp.zeros((), jnp.bfloat16)
    send_k = jnp.where(filled, jnp.take(cache_k, picked, axis=0), zero_block)
    send_v = jnp.where(filled, jnp.take(cache_v, picked, axis=0), zero_block)
    recv_k, recv_v = (
        lax.all_to_all(send_k, "grp", split_axis=0, concat_axis=0, tiled=True),
        lax.all_to_all(send_v, "grp", split_axis=0, concat_axis=0, tiled=True),
    )
    my_source = lax.dynamic_slice_in_dim(source, first_slot, per_group)
    source_group = my_source // per_group
    arrival = per_group + source_group * MOVE + jnp.take(mover_rank, my_source)
    where_from = jnp.where(source_group == group_id, my_source - first_slot, arrival)
    moved_k = jnp.take(jnp.concatenate([cache_k, recv_k], axis=0), where_from, axis=0)
    moved_v = jnp.take(jnp.concatenate([cache_v, recv_v], axis=0), where_from, axis=0)
    positions = dev_id * block_len + jnp.arange(block_len, dtype=jnp.int32)
    hit = (positions[None, :] == lengths[:, None])[:, None, :, None]
    new_cache_k = jnp.where(hit, new_key[:, :, None, :], moved_k)
    new_cache_v = jnp.where(hit, new_value[:, :, None, :], moved_v)
    share_heads = query.shape[1] // (kv_heads * head_dim)
    grouped = query.reshape(per_group, kv_heads, share_heads, head_dim)
    scores = (
        jnp.einsum("rkgh,rkph->rkgp", grouped, new_cache_k, preferred_element_type=jnp.float32)
        / head_dim**0.5
    )
    valid = (positions[None, :] <= lengths[:, None])[:, None, None, :]
    scores = jnp.where(valid, scores, jnp.float32(-1e30))
    local_peak = jnp.max(scores, axis=-1)
    values_wide = new_cache_v.astype(jnp.float32)
    peak = lax.pmax(local_peak, "dev")
    weights = jnp.where(valid, jnp.exp(scores - peak[..., None]), jnp.float32(0.0))
    local_total = jnp.sum(weights, axis=-1)
    local_context = jnp.einsum(
        "rkgp,rkph->rkgh", weights, values_wide, precision=lax.Precision.HIGHEST
    )
    totals, context = (
        lax.psum(local_total.astype(jnp.bfloat16), "dev").astype(jnp.float32),
        lax.psum(local_context.astype(jnp.bfloat16), "dev").astype(jnp.float32),
    )
    attn = (context / totals[..., None]).reshape(per_group, -1).astype(jnp.bfloat16)
    row_count = out_weight.shape[0]
    attn_mine = lax.dynamic_slice_in_dim(attn, dev_id * row_count, row_count, 1)
    partial_value = jnp.dot(attn_mine, out_weight, preferred_element_type=jnp.float32)
    expert_range = jnp.arange(EXPERTS, dtype=jnp.int32)
    onehot = expert_ids[:, :, None] == expert_range[None, None, :]
    flat_hot = onehot.reshape(per_group * TOP, EXPERTS).astype(jnp.int32)
    before = jnp.cumsum(flat_hot, axis=0) - flat_hot
    route_rank = jnp.sum(before * flat_hot, axis=1).reshape(per_group, TOP)
    slot_hot = (route_rank[:, :, None] == jnp.arange(CAP, dtype=jnp.int32)[None, None, :]).astype(
        jnp.float32
    )
    codes = gate_codes.astype(jnp.float32)
    gate_weight = codes / jnp.sum(codes, axis=-1, keepdims=True)
    selector = jnp.einsum("tke,tkc->ect", onehot.astype(jnp.float32), slot_hot)
    weighted_sel = jnp.einsum("tke,tkc,tk->ect", onehot.astype(jnp.float32), slot_hot, gate_weight)
    col_start = dev_id * feat_width
    split = group_count * dev_count // EXPERTS
    share = lax.psum_scatter(
        partial_value.astype(jnp.bfloat16), "dev", scatter_dimension=1, tiled=True
    ).astype(jnp.float32)
    mixed = resid.astype(jnp.float32) + share
    total_sq = lax.psum(jnp.sum(mixed * mixed, axis=1), "dev")
    gain_mine = lax.dynamic_slice_in_dim(norm_gain, col_start, feat_width).astype(jnp.float32)
    normed = (
        mixed * lax.rsqrt(total_sq / model_width + 1e-05)[:, None] * gain_mine[None, :]
    ).astype(jnp.bfloat16)
    slot_rows = jnp.einsum(
        "ect,tf->ecf", selector.astype(jnp.bfloat16), normed, preferred_element_type=jnp.float32
    ).astype(jnp.bfloat16)
    send_rows = jnp.broadcast_to(slot_rows[:, None], (EXPERTS, split, CAP, feat_width)).reshape(
        group_count * dev_count, CAP, feat_width
    )
    received = lax.all_to_all(send_rows, ("grp", "dev"), split_axis=0, concat_axis=0, tiled=True)
    slot_count = received.shape[1]
    rows = (
        received.reshape(group_count, dev_count, slot_count, feat_width)
        .transpose(0, 2, 1, 3)
        .reshape(group_count * slot_count, model_width)
    )
    outputs = expert_ffn(rows, w_gate, w_up, w_down)
    back = (
        outputs.reshape(group_count, slot_count, dev_count, feat_width)
        .transpose(0, 2, 1, 3)
        .reshape(group_count * dev_count, slot_count, feat_width)
    )
    returned = lax.all_to_all(
        back.astype(jnp.bfloat16), ("grp", "dev"), split_axis=0, concat_axis=0, tiled=True
    ).astype(back.dtype)
    expert_sums = jnp.sum(returned.reshape(EXPERTS, split, CAP, feat_width), axis=1)
    moe = jnp.einsum("ect,ecf->tf", weighted_sel, expert_sums, precision=lax.Precision.HIGHEST)
    layer_out = (mixed + moe).astype(jnp.bfloat16)
    return (new_cache_k, new_cache_v, layer_out)


def solution(mesh):
    in_specs = (
        P("grp", None, "dev", None),
        P("grp", None, "dev", None),
        P(),
        P("grp"),
        P("grp", None),
        P("grp", None, None),
        P("grp", None, None),
        P("grp", "dev"),
        P("dev", None),
        P(),
        P(None, ("grp", "dev")),
        P(None, ("grp", "dev")),
        P(("grp", "dev"), None),
        P("grp", None),
        P("grp", None),
    )
    out_specs = (P("grp", None, "dev", None), P("grp", None, "dev", None), P("grp", "dev"))
    return jax.shard_map(
        on_device, mesh=mesh, in_specs=in_specs, out_specs=out_specs, check_vma=False
    )
```

profile of v0, /device:TPU:1, one launch (start us, length us, event | category | flops | bytes accessed | tf_op | source)
XLA Modules:
  0.0 510.9 jit_solution(866724259967790486)
XLA Ops:
  7.2 0.9 select_reduce_fusion
  8.9 2.6 gather_fusion.1
  11.6 2.7 gather_fusion.3
  14.2 2.4 select_select_fusion.2
  16.7 4.8 all-to-all-start
  22.9 7.1 %all-to-all-done = bf16[8,8,32,128]{3,2,1,0:T(8,128)(2,1)} async-done(((bf16[8,8,32,128]{3,2,1,0:T(8,128)(2,1)}), bf16[8,8,32,128]{3,2,1,0:T(8,128)(2,1)}, u32[]{:S(2)}, u32[]{:S(2)}) %all-to-all-start) | async-done | bytes 524320 | tf_op jit(solution)/shard_map/all_to_all | solution.py:73
  29.9 4.1 all-to-all-start.1
  34.1 1.9 reshape.201
  36.2 2.3 pad_maximum_fusion
  38.6 2.2 gather_fusion.2
  41.3 2.7 pad_maximum_fusion.1
  44.0 3.1 gather_fusion.4
  47.1 2.5 select_select_fusion
  49.6 1.0 copy-done.1
  51.3 125.5 %pmax.7 = f32[16,8,6]{2,1,0:T(8,128)S(1)} all-reduce(f32[16,8,6]{2,1,0:T(8,128)S(1)} %get-tuple-element.15), channel_id=1, replica_groups=mesh['grp'=4,'dev'=32] {'dev'}, use_global_device_ids=true, to_apply=%region_5.8 | all-reduce | flops 768 | bytes 6144 | tf_op jit(solution)/shard_map/pmax | solution.py:96
  176.9 2.9 convolution_convert_fusion.2
  180.3 123.9 %psum.22 = bf16[16,8,6]{2,1,0:T(8,128)(2,1)S(1)} all-reduce(bf16[16,8,6]{2,1,0:T(8,128)(2,1)S(1)} %fusion.6), channel_id=1, replica_groups=mesh['grp'=4,'dev'=32] {'dev'}, use_global_device_ids=true, to_apply=%region_8.11 | all-reduce | flops 768 | bytes 3072 | tf_op jit(solution)/shard_map/psum | solution.py:103
  304.2 1.2 divide_convert_fusion
  306.1 1.5 copy.47
  308.6 76.5 %reduce-scatter.4.cloned.1.call-done = bf16[192,16]{1,0:T(8,128)(2,1)} async-done(((bf16[6144,16]{1,0:T(8,128)(2,1)}), bf16[192,16]{1,0:T(8,128)(2,1)}) %reduce-scatter.4.cloned.1.call-update) | async-done | bytes 6160
  385.1 0.9 copy.48
  386.2 64.4 %psum.23 = f32[16]{0:T(128)S(1)} all-reduce(f32[16]{0:T(128)S(1)} %multiply_reduce_fusion), channel_id=1, replica_groups=mesh['grp'=4,'dev'=32] {'dev'}, use_global_device_ids=true, to_apply=%region_14.17 | all-reduce | flops 16 | bytes 128 | tf_op jit(solution)/shard_map/psum | solution.py:128
  450.8 0.8 broadcast_in_dim.162
  451.6 4.7 all-to-all-start.2
  456.4 13.5 %all-to-all-done.2 = bf16[128,8,192]{2,1,0:T(8,128)(2,1)S(1)} async-done(((bf16[128,8,192]{2,1,0:T(8,128)(2,1)}), bf16[128,8,192]{2,1,0:T(8,128)(2,1)S(1)}, u32[]{:S(2)}, u32[]{:S(2)}) %all-to-all-start.2) | async-done | bytes 393248 | tf_op jit(solution)/shard_map/all_to_all | solution.py:139
  470.6 1.2 copy.44
  472.3 3.9 fusion.38
  476.3 7.0 %convolution_convert_fusion = bf16[32,6144]{1,0:T(8,128)(2,1)S(1)} fusion(bf16[512,6144]{1,0:T(8,128)(2,1)} %param.31, bf16[32,6144]{1,0:T(8,128)(2,1)S(1)} %reshape.204, bf16[6144,512]{1,0:T(8,128)(2,1)} %param.30, f32[32,512]{1,0:T(8,128)S(1)} %fusion.38), kind=kOutput, calls=%fused_computation.5 | convolution fusion | flops 402948096 | bytes 13434880 | tf_op jit(solution)/shard_map/dot_general | solution.py:16
  483.8 1.1 copy.45
  484.9 4.8 all-to-all-start.3
  490.3 12.9 %all-to-all-done.3 = bf16[128,8,192]{2,1,0:T(8,128)(2,1)S(1)} async-done(((bf16[128,8,192]{2,1,0:T(8,128)(2,1)}), bf16[128,8,192]{2,1,0:T(8,128)(2,1)S(1)}, u32[]{:S(2)}, u32[]{:S(2)}) %all-to-all-start.3) | async-done | bytes 393248 | tf_op jit(solution)/shard_map/all_to_all | solution.py:152
  503.3 0.8 fusion.5
  (73 shorter events, 9.1 us)
Async XLA Ops:
  7.2 298.4 %copy-start = (bf16[192,6144]{1,0:T(8,128)(2,1)S(1)}, bf16[192,6144]{1,0:T(8,128)(2,1)}, u32[]{:S(2)}) copy-start(bf16[192,6144]{1,0:T(8,128)(2,1)} %param.27) | copy-start | bytes 7077892
  11.6 9.9 %copy-start.10 = (s32[64]{0:T(128)S(1)}, s32[64]{0:T(128)}, u32[]{:S(2)}) copy-start(s32[64]{0:T(128)} %param.21) | copy-start | bytes 772
  11.6 10.7 %copy-start.8 = (s32[16,2]{0,1:T(2,128)S(1)}, s32[16,2]{0,1:T(2,128)}, u32[]{:S(2)}) copy-start(s32[16,2]{0,1:T(2,128)} %param.32) | copy-start | bytes 388
  14.2 21.9 %copy-start.11 = (s32[16]{0:T(128)S(1)}, s32[16]{0:T(128)}, u32[]{:S(2)}) copy-start(s32[16]{0:T(128)} %param.22) | copy-start | bytes 196
  14.2 22.0 %copy-start.2 = (bf16[16,8,32,128]{3,2,1,0:T(8,128)(2,1)S(1)}, bf16[16,8,32,128]{3,2,1,0:T(8,128)(2,1)}, u32[]{:S(2)}) copy-start(bf16[16,8,32,128]{3,2,1,0:T(8,128)(2,1)} %param.19) | copy-start | bytes 3145732
  16.7 13.3 %all-to-all-start = ((bf16[8,8,32,128]{3,2,1,0:T(8,128)(2,1)}), bf16[8,8,32,128]{3,2,1,0:T(8,128)(2,1)}, u32[]{:S(2)}, u32[]{:S(2)}) async-start(bf16[8,8,32,128]{3,2,1,0:T(8,128)(2,1)} %get-tuple-element.14), calls=%async_computation | async-start | bytes 1048576 | tf_op jit(solution)/shard_map/all_to_all | solution.py:73
  29.9 11.4 %all-to-all-start.1 = ((bf16[8,8,32,128]{3,2,1,0:T(8,128)(2,1)}), bf16[8,8,32,128]{3,2,1,0:T(8,128)(2,1)}, u32[]{:S(2)}, u32[]{:S(2)}) async-start(bf16[8,8,32,128]{3,2,1,0:T(8,128)(2,1)} %get-tuple-element.13), calls=%async_computation.1 | async-start | bytes 1048576 | tf_op jit(solution)/shard_map/all_to_all | solution.py:74
  34.1 270.1 %all-reduce.2.cloned.1.call-start = ((), (), s32[]{:S(2)}) async-start(), calls=%async_computation.5 | async-start | bytes 524288 | tf_op jit(solution)/shard_map/psum | solution.py:104
  40.7 6.3 %copy-start.6 = (bf16[16,8,128]{2,1,0:T(8,128)(2,1)S(1)}, bf16[16,8,128]{2,1,0:T(8,128)(2,1)}, u32[]{:S(2)}) copy-start(bf16[16,8,128]{2,1,0:T(8,128)(2,1)} %param.25) | copy-start | bytes 98308
  40.7 6.3 %copy-start.7 = (bf16[16,8,128]{2,1,0:T(8,128)(2,1)S(1)}, bf16[16,8,128]{2,1,0:T(8,128)(2,1)}, u32[]{:S(2)}) copy-start(bf16[16,8,128]{2,1,0:T(8,128)(2,1)} %param.24) | copy-start | bytes 98308
  47.1 3.5 copy-start.4
  49.6 1.0 copy-start.1
  179.8 205.3 %reduce-scatter.4.cloned.1.call-start = ((), (), s32[]{:S(2)}) async-start(), calls=%async_computation.6 | async-start | bytes 1622016
  306.0 79.9 %copy-start.5 = (bf16[16,192]{1,0:T(8,128)(2,1)S(1)}, bf16[16,192]{1,0:T(8,128)(2,1)}, u32[]{:S(2)}) copy-start(bf16[16,192]{1,0:T(8,128)(2,1)} %param.26) | copy-start | bytes 18436
  306.0 150.3 %copy-start.9 = (s32[16,2]{0,1:T(2,128)S(1)}, s32[16,2]{0,1:T(2,128)}, u32[]{:S(2)}) copy-start(s32[16,2]{0,1:T(2,128)} %param.33) | copy-start | bytes 388
  451.6 18.2 %all-to-all-start.2 = ((bf16[128,8,192]{2,1,0:T(8,128)(2,1)}), bf16[128,8,192]{2,1,0:T(8,128)(2,1)S(1)}, u32[]{:S(2)}, u32[]{:S(2)}) async-start(bf16[128,8,192]{2,1,0:T(8,128)(2,1)} %bitcast.4), calls=%async_computation.2 | async-start | bytes 1048576 | tf_op jit(solution)/shard_map/all_to_all | solution.py:139
  469.8 0.8 copy-start.3
  484.9 18.3 %all-to-all-start.3 = ((bf16[128,8,192]{2,1,0:T(8,128)(2,1)}), bf16[128,8,192]{2,1,0:T(8,128)(2,1)S(1)}, u32[]{:S(2)}, u32[]{:S(2)}) async-start(bf16[128,8,192]{2,1,0:T(8,128)(2,1)} %bitcast.8), calls=%async_computation.3 | async-start | bytes 1048576 | tf_op jit(solution)/shard_map/all_to_all | solution.py:152
Sparse Core Ops, SparseCore 0:
  179.9 102.9 all-reduce.1
  307.7 77.3 reduce-scatter.3
where the time goes:
time: 512 us; the launch traced here: 511 us
  blocking collectives  314 us (61%)
  waiting for transfers between devices  111 us (22%)
  local copies, waits for them, and re-layouts  22.5 us (4%)
  starting transfers between devices  18.5 us (4%)
  matrix products  16.7 us (3%)
  other arithmetic  14.7 us (3%)
  between operations  14.3 us (3%)
    pmax x1, blocking collectives, on_device(): peak = lax.pmax(local_peak, 'dev')  126 us
    psum x1, blocking collectives, on_device(): lax.psum(local_total.astype(jnp.bfloat16), 'dev').astype(jnp.float32)  124 us
    unnamed x3, waiting for transfers between devices  76.5 us
    psum x1, blocking collectives, on_device(): total_sq = lax.psum(jnp.sum(mixed * mixed, axis=1), 'dev')  64.4 us
    all_to_all x1, waiting for transfers between devices, on_device(): lax.all_to_all(send_rows, ('grp', 'dev'), split_axis=0, concat_axis=0, ti...  13.5 us
    all_to_all x1, waiting for transfers between devices, on_device(): lax.all_to_all(back.astype(jnp.bfloat16), ('grp', 'dev'), split_axis=0, c...  12.9 us
  transfers between devices with their start and end apart: 6, of which 5 were waited for; matrix products, arithmetic and copies ran while one was open for 2% of the time, Pallas kernels for 0%

commit v1 on v0

v1 whole, which is shorter than its diff:
```python
import functools

import jax
import jax.numpy as jnp
from jax import lax
from jax.experimental import pallas as pl
from jax.experimental.pallas import tpu as pltpu
from jax.sharding import PartitionSpec as P

EXPERTS = 8
MOVE = 2
CAP = 8
LANES = 128
HALF = 64
F32 = jnp.float32
BF16 = jnp.bfloat16
VMEM = pl.BlockSpec(memory_space=pltpu.VMEM)
SMEM = pl.BlockSpec(memory_space=pltpu.SMEM)
ANY = pl.BlockSpec(memory_space=pl.ANY)


def pieces(value, count):
    terms = []
    for _ in range(count):
        term = value.astype(BF16).astype(F32)
        terms.append(term)
        value = value - term
    return terms


def iota(shape, dim):
    return lax.broadcasted_iota(jnp.int32, shape, dim)


def pack_kernel(groups, per, src, cache_k, cache_v, out, sem):
    me = lax.axis_index("grp")
    copies = []
    for dest in range(groups):
        count = jnp.int32(0)
        picks = [jnp.int32(0)] * MOVE
        for slot in range(per):
            old = src[dest * per + slot]
            mine = (old // per == me) & (me != dest)
            for rank in range(MOVE):
                picks[rank] = jnp.where(mine & (count == rank), old % per, picks[rank])
            count = count + mine.astype(jnp.int32)
        for rank in range(MOVE):
            for which, cache in ((0, cache_k), (1, cache_v)):
                copy = pltpu.make_async_copy(
                    cache.at[picks[rank]], out.at[dest, which, rank], sem.at[dest, which, rank]
                )
                copy.start()
                copies.append(copy)
    for copy in copies:
        copy.wait()


def attend_kernel(
    groups, per, src, length, cache_k, cache_v, recv, query, new_key, new_value,
    out_k, out_v, ctx, kbuf, vbuf, in_sem, out_sem,
):
    me = lax.axis_index("grp")
    dev = lax.axis_index("dev")
    heads_kv, block = kbuf.shape[1], kbuf.shape[2]
    share = query.shape[0] // heads_kv
    base = dev * block
    counts = [jnp.int32(0)] * groups
    for slot in range(per):
        old = src[me * per + slot]
        owner = old // per
        stays = owner == me
        rank = jnp.int32(0)
        for g in range(groups):
            here = owner == g
            rank = jnp.where(here, counts[g], rank)
            counts[g] = counts[g] + here.astype(jnp.int32)
        rank = jnp.minimum(rank, MOVE - 1)

        @pl.when(stays)
        def _():
            pltpu.make_async_copy(cache_k.at[old % per], kbuf.at[slot], in_sem.at[0, slot]).start()
            pltpu.make_async_copy(cache_v.at[old % per], vbuf.at[slot], in_sem.at[1, slot]).start()

        @pl.when(jnp.logical_not(stays))
        def _():
            pltpu.make_async_copy(recv.at[owner, 0, rank], kbuf.at[slot], in_sem.at[0, slot]).start()
            pltpu.make_async_copy(recv.at[owner, 1, rank], vbuf.at[slot], in_sem.at[1, slot]).start()

    col = iota((per, per * block), 1)
    row = iota((per, per * block), 0)
    limit = jnp.full((per, per * block), -1, jnp.int32)
    for slot in range(per):
        limit = jnp.where(row == slot, length[slot] - base, limit)
    valid = (col // block == row) & (col % block <= limit)

    outs = []
    for slot in range(per):
        pltpu.make_async_copy(cache_k.at[0], kbuf.at[slot], in_sem.at[0, slot]).wait()
        pltpu.make_async_copy(cache_v.at[0], vbuf.at[slot], in_sem.at[1, slot]).wait()
        spot = length[slot] - base

        @pl.when((spot >= 0) & (spot < block))
        def _():
            hit = iota((heads_kv, block, LANES), 1) == spot
            kbuf[slot] = jnp.where(hit, new_key[slot][:, None, :], kbuf[slot])
            vbuf[slot] = jnp.where(hit, new_value[slot][:, None, :], vbuf[slot])

        for which, buf, out in ((0, kbuf, out_k), (1, vbuf, out_v)):
            copy = pltpu.make_async_copy(buf.at[slot], out.at[slot], out_sem.at[which, slot])
            copy.start()
            outs.append(copy)

    lane = iota((1, 1, LANES), 2)
    scale = LANES**-0.5
    tiles, stats = [], []
    for kv in range(heads_kv):
        keys = kbuf[:, kv].reshape(per * block, LANES)
        values = vbuf[:, kv].reshape(per * block, LANES)
        rows = query[kv * share : (kv + 1) * share].reshape(share * per, LANES)
        scores = lax.dot_general(
            rows, keys, (((1,), (1,)), ((), ())), preferred_element_type=F32
        ).reshape(share, per, per * block) * scale
        scores = jnp.where(valid[None], scores, F32(-1e30))
        peak = jnp.max(scores, axis=-1, keepdims=True)
        weights = jnp.where(valid[None], jnp.exp(scores - peak), F32(0.0)).astype(BF16)
        total = jnp.sum(weights.astype(F32), axis=-1, keepdims=True)
        context = jnp.dot(
            weights.reshape(share * per, per * block), values, preferred_element_type=F32
        ).reshape(share, per, LANES)
        terms = pieces(peak, 3) + pieces(total, 2)
        stat = jnp.zeros((share, per, LANES), F32)
        for at, term in enumerate(terms):
            stat = jnp.where(lane % 8 == at, term, stat)
        for h in range(share):
            tiles.append(context[h])
            stats.append(stat[h])
    lane = iota((per, LANES), 1)
    first = (lane // 8) % 2 == 0
    low = lane < HALF
    for m in range(len(tiles) // 3):
        a, b, c = tiles[3 * m : 3 * m + 3]
        sa, sb, sc = stats[3 * m : 3 * m + 3]
        ctx[2 * m, 0] = a.astype(BF16)
        ctx[2 * m, 1] = jnp.where(low, b, jnp.where(first, sa, sb)).astype(BF16)
        ctx[2 * m + 1, 0] = jnp.where(low, jnp.where(first, sb, sc), b).astype(BF16)
        ctx[2 * m + 1, 1] = c.astype(BF16)
    for copy in outs:
        copy.wait()


def project_kernel(recv, weight, out):
    even = lax.axis_index("dev") % 2 == 0
    per = recv.shape[2]
    stat = jnp.where(even, recv[:, 1, :, HALF : HALF + 16], recv[:, 0, :, 0:16]).astype(F32)
    parts = []
    for k in range(2):
        at = 8 * k
        peak = stat[..., at : at + 1] + stat[..., at + 1 : at + 2] + stat[..., at + 2 : at + 3]
        total = stat[..., at + 3 : at + 4] + stat[..., at + 4 : at + 5]
        top = jnp.max(peak, axis=0, keepdims=True)
        factor = jnp.exp(peak - top)
        whole = jnp.sum(factor * total, axis=0)
        parts.append(jnp.sum(factor * recv[:, k].astype(F32), axis=0) / whole)
    both = jnp.concatenate(parts, axis=1)
    rows = weight.shape[0]
    attn = jnp.where(even, both[:, :rows], both[:, 2 * LANES - rows :]).astype(BF16)
    for m in range(out.shape[0] // 2):
        part = jnp.dot(
            attn, weight[:, 3 * LANES * m : 3 * LANES * (m + 1)], preferred_element_type=F32
        ).astype(BF16)
        t0, t1, t2 = (part[:, LANES * j : LANES * (j + 1)] for j in range(3))
        out[2 * m, 0] = t0
        out[2 * m, 1] = t1
        out[2 * m + 1, 0] = t1
        out[2 * m + 1, 1] = t2


def tiles_of(even, wide):
    rows = wide.shape[0]
    zero = jnp.zeros((rows, HALF), wide.dtype)
    left = jnp.concatenate([wide, zero], axis=1)
    right = jnp.concatenate([zero, wide], axis=1)
    both = jnp.where(even, left, right)
    return both[:, :LANES], both[:, LANES:]


def dispatch_kernel(recv, resid, gain, qrow, mixed, out):
    dev = lax.axis_index("dev")
    even = dev % 2 == 0
    per = recv.shape[2]
    lane = iota((per, LANES), 1)
    spare = (even & (lane >= HALF), jnp.logical_not(even) & (lane < HALF))
    spare = (spare[1], spare[0])
    start = tiles_of(even, resid[...].astype(F32))
    square = jnp.zeros((per, 1), F32)
    wides = []
    for k in range(2):
        part = start[k] + jnp.sum(recv[:, k].astype(F32), axis=0)
        part = jnp.where(spare[k], F32(0.0), part)
        mixed[k] = part
        square = square + jnp.sum(part * part, axis=1, keepdims=True)
        at = 3 * (dev // 2) + dev % 2 + k
        own = jnp.where(iota(gain.shape, 0) == at, gain[...].astype(F32), F32(0.0))
        wides.append(part * jnp.sum(own, axis=0, keepdims=True))
    stat = jnp.zeros((per, LANES), F32)
    for at, term in enumerate(pieces(square, 3)):
        stat = jnp.where(lane % 8 == at, term, stat)
    rows = jnp.concatenate(
        [jnp.where(spare[k], stat, wides[k]).astype(BF16) for k in range(2)], axis=0
    )
    count = EXPERTS * 2 * CAP
    where = iota((count, 2 * per), 0)
    from_ = iota((count, 2 * per), 1)
    slot = (where // (2 * CAP)) * CAP + where % CAP
    named = (slot == qrow[0:1, :]) | (slot == qrow[1:2, :])
    pick = (named & ((where // CAP) % 2 == from_ // per)).astype(F32).astype(BF16)
    sent = jnp.dot(pick, rows, preferred_element_type=F32).astype(BF16)
    split = out.shape[0] // EXPERTS
    for e in range(EXPERTS):
        block = sent[2 * CAP * e : 2 * CAP * (e + 1)]
        for s in range(split):
            out[e * split + s] = block


def expert_kernel(groups, recv, w_gate, w_up, w_down, out, xbuf, wg, wu, wd, sem):
    width = xbuf.shape[1]
    chunks = wg.shape[0]
    depth = wg.shape[1]
    copies = []
    for j in range(chunks):
        pair = []
        for which, (src, dst) in enumerate(((w_gate, wg), (w_up, wu))):
            copy = pltpu.make_async_copy(
                src.at[pl.ds(j * depth, depth), :], dst.at[j], sem.at[which, j]
            )
            copy.start()
            pair.append(copy)
        copies.append(pair)
    down_chunks = wd.shape[0]
    span = wd.shape[2]
    downs = []
    for j in range(down_chunks):
        copy = pltpu.make_async_copy(
            w_down.at[:, pl.ds(j * span, span)], wd.at[j], sem.at[2, j]
        )
        copy.start()
        downs.append(copy)
    devs = recv.shape[0] // groups
    lane = iota((CAP, LANES), 1)
    low = lane < HALF
    rows_square = []
    for g in range(groups):
        acc = jnp.zeros((CAP, LANES), F32)
        for m in range(devs // 2):
            e, o = recv[g * devs + 2 * m], recv[g * devs + 2 * m + 1]
            middle_e, middle_o = e[CAP:].astype(F32), o[:CAP].astype(F32)
            acc = acc + jnp.where(low, middle_o, middle_e)
            at = slice(CAP * g, CAP * (g + 1))
            xbuf[at, 3 * LANES * m : 3 * LANES * m + LANES] = e[:CAP]
            xbuf[at, 3 * LANES * m + LANES : 3 * LANES * m + 2 * LANES] = jnp.where(
                low, middle_e, middle_o
            ).astype(BF16)
            xbuf[at, 3 * LANES * m + 2 * LANES : 3 * LANES * (m + 1)] = o[CAP:]
        both = acc[:, :8] + acc[:, HALF : HALF + 8]
        rows_square.append(both[:, 0:1] + both[:, 1:2] + both[:, 2:3])
    square = jnp.concatenate(rows_square, axis=0)
    scale = lax.rsqrt(square / width + 1e-05)
    gate = jnp.zeros((groups * CAP, wg.shape[2]), F32)
    up = jnp.zeros((groups * CAP, wu.shape[2]), F32)
    for j in range(chunks):
        for copy in copies[j]:
            copy.wait()
        x = xbuf[:, depth * j : depth * (j + 1)]
        gate = gate + jnp.dot(x, wg[j], preferred_element_type=F32)
        up = up + jnp.dot(x, wu[j], preferred_element_type=F32)
    gate, up = gate * scale, up * scale
    hidden = (gate / (1.0 + jnp.exp(-gate)) * up).astype(BF16)
    per_chunk = span // (3 * LANES)
    for j in range(down_chunks):
        downs[j].wait()
        part = jnp.dot(hidden, wd[j], preferred_element_type=F32)
        for i in range(per_chunk):
            m = j * per_chunk + i
            t = [
                part[:, 3 * LANES * i + LANES * k : 3 * LANES * i + LANES * (k + 1)]
                for k in range(3)
            ]
            for g in range(groups):
                at = slice(CAP * g, CAP * (g + 1))
                out[g * devs + 2 * m] = jnp.concatenate([t[0][at], t[1][at]], axis=0).astype(BF16)
                out[g * devs + 2 * m + 1] = jnp.concatenate([t[1][at], t[2][at]], axis=0).astype(
                    BF16
                )


def final_kernel(recv, mixed, qcol, share, out):
    even = lax.axis_index("dev") % 2 == 0
    split = recv.shape[0] // EXPERTS
    per = mixed.shape[1]
    sums = [
        jnp.sum(recv[e * split : (e + 1) * split].astype(F32), axis=0) for e in range(EXPERTS)
    ]
    slot = iota((per, EXPERTS * CAP), 1)
    weight = jnp.where(slot == qcol[:, 0:1], share[:, 0:1], F32(0.0)) + jnp.where(
        slot == qcol[:, 1:2], share[:, 1:2], F32(0.0)
    )
    done = []
    for k in range(2):
        expert = jnp.concatenate([s[CAP * k : CAP * (k + 1)] for s in sums], axis=0)
        moe = jnp.dot(
            weight, expert, preferred_element_type=F32, precision=lax.Precision.HIGHEST
        )
        done.append(mixed[k] + moe)
    both = jnp.concatenate(done, axis=1)
    width = out.shape[1]
    out[...] = jnp.where(even, both[:, :width], both[:, 2 * LANES - width :]).astype(BF16)


def params(mib):
    return pltpu.CompilerParams(vmem_limit_bytes=mib << 20)


def on_device(
    cache_k,
    cache_v,
    source,
    lengths,
    query,
    new_key,
    new_value,
    resid,
    out_weight,
    norm_gain,
    w_gate,
    w_up,
    w_down,
    expert_ids,
    gate_codes,
):
    groups = lax.axis_size("grp")
    devs = lax.axis_size("dev")
    per, kv_heads, block, head_dim = cache_k.shape
    heads = query.shape[1] // head_dim
    width = query.shape[1]
    hidden = w_gate.shape[1]
    sds = jax.ShapeDtypeStruct
    move_shape = (groups, 2, MOVE, kv_heads, block, head_dim)

    sent = pl.pallas_call(
        functools.partial(pack_kernel, groups, per),
        name="pack",
        out_shape=sds(move_shape, BF16),
        in_specs=[SMEM, ANY, ANY],
        out_specs=VMEM,
        scratch_shapes=[pltpu.SemaphoreType.DMA((groups, 2, MOVE))],
        compiler_params=params(8),
    )(source, cache_k, cache_v)
    moved = lax.all_to_all(sent, "grp", split_axis=0, concat_axis=0, tiled=True)

    flat = expert_ids.reshape(-1)
    order = jnp.arange(flat.shape[0], dtype=jnp.int32)
    same = (flat[:, None] == flat[None, :]) & (order[None, :] < order[:, None])
    qflat = flat * CAP + jnp.sum(same.astype(jnp.int32), axis=1)
    qcol = qflat.reshape(per, 2)
    qrow = jnp.concatenate([qcol.T, qcol.T], axis=1)
    codes = gate_codes.astype(F32)
    share = codes / jnp.sum(codes, axis=-1, keepdims=True)
    by_head = query.reshape(per, heads, head_dim).transpose(1, 0, 2)

    new_k, new_v, ctx = pl.pallas_call(
        functools.partial(attend_kernel, groups, per),
        name="attend",
        out_shape=(
            sds(cache_k.shape, BF16),
            sds(cache_v.shape, BF16),
            sds((devs, 2, per, LANES), BF16),
        ),
        in_specs=[SMEM, SMEM, ANY, ANY, ANY, VMEM, VMEM, VMEM],
        out_specs=(ANY, ANY, VMEM),
        scratch_shapes=[
            pltpu.VMEM(cache_k.shape, BF16),
            pltpu.VMEM(cache_v.shape, BF16),
            pltpu.SemaphoreType.DMA((2, per)),
            pltpu.SemaphoreType.DMA((2, per)),
        ],
        compiler_params=params(16),
    )(source, lengths, cache_k, cache_v, moved, by_head, new_key, new_value)
    ctx = lax.all_to_all(ctx, "dev", split_axis=0, concat_axis=0, tiled=True)

    partial_rows = pl.pallas_call(
        project_kernel,
        name="project",
        out_shape=sds((devs, 2, per, LANES), BF16),
        in_specs=[VMEM, VMEM],
        out_specs=VMEM,
        compiler_params=params(12),
    )(ctx, out_weight)
    partial_rows = lax.all_to_all(partial_rows, "dev", split_axis=0, concat_axis=0, tiled=True)

    mixed, rows = pl.pallas_call(
        dispatch_kernel,
        name="dispatch",
        out_shape=(
            sds((2, per, LANES), F32),
            sds((groups * devs, 2 * CAP, LANES), BF16),
        ),
        in_specs=[VMEM] * 4,
        out_specs=(VMEM, VMEM),
        compiler_params=params(8),
    )(partial_rows, resid, norm_gain.reshape(-1, LANES), qrow)
    rows = lax.all_to_all(rows, ("grp", "dev"), split_axis=0, concat_axis=0, tiled=True)

    chunks, down_chunks = 8, 4
    partial_out = pl.pallas_call(
        functools.partial(expert_kernel, groups),
        name="expert",
        out_shape=sds((groups * devs, 2 * CAP, LANES), BF16),
        in_specs=[VMEM, ANY, ANY, ANY],
        out_specs=VMEM,
        scratch_shapes=[
            pltpu.VMEM((groups * CAP, width), BF16),
            pltpu.VMEM((chunks, width // chunks, hidden), BF16),
            pltpu.VMEM((chunks, width // chunks, hidden), BF16),
            pltpu.VMEM((down_chunks, hidden, width // down_chunks), BF16),
            pltpu.SemaphoreType.DMA((3, chunks)),
        ],
        compiler_params=params(32),
    )(rows, w_gate, w_up, w_down)
    partial_out = lax.all_to_all(
        partial_out, ("grp", "dev"), split_axis=0, concat_axis=0, tiled=True
    )

    layer_out = pl.pallas_call(
        final_kernel,
        name="final",
        out_shape=sds(resid.shape, BF16),
        in_specs=[VMEM] * 4,
        out_specs=VMEM,
        compiler_params=params(8),
    )(partial_out, mixed, qcol, share)
    return (new_k, new_v, layer_out)


def solution(mesh):
    in_specs = (
        P("grp", None, "dev", None),
        P("grp", None, "dev", None),
        P(),
        P("grp"),
        P("grp", None),
        P("grp", None, None),
        P("grp", None, None),
        P("grp", "dev"),
        P("dev", None),
        P(),
        P(None, ("grp", "dev")),
        P(None, ("grp", "dev")),
        P(("grp", "dev"), None),
        P("grp", None),
        P("grp", None),
    )
    out_specs = (P("grp", None, "dev", None), P("grp", None, "dev", None), P("grp", "dev"))
    return jax.shard_map(
        on_device, mesh=mesh, in_specs=in_specs, out_specs=out_specs, check_vma=False
    )
```

time: 512 us -> 125 us (0.24)
  blocking collectives: 314 us -> 17.1 us
  waiting for transfers between devices: 111 us -> 44.4 us
  Pallas kernels: 0 us -> 19.4 us
  matrix products: 16.7 us -> 0 us
  other arithmetic: 14.7 us -> 0.46 us
  between operations: 14.3 us -> 0.78 us
    psum x2 -> x0, blocking collectives: 188 us -> none  [the longest x1 124 us: on_device(): lax.psum(local_total.astype(jnp.bfloat16), 'dev').astype(jnp.float32)]
    pmax x1 -> x0, blocking collectives: 126 us -> none  [on_device(): peak = lax.pmax(local_peak, 'dev')]
    unnamed x3 -> x0, waiting for transfers between devices: 76.5 us -> none
    pallas_call x0 -> x6, Pallas kernels: none -> 19.4 us  [the longest x1 6.96 us: on_device(): pl.pallas_call(functools.partial(expert_kernel, groups), name='expert', o...]
    all_to_all x0 -> x1, blocking collectives: none -> 17.1 us  [on_device(): lax.all_to_all(rows, ('grp', 'dev'), split_axis=0, concat_axis=0, tiled=T...]
    dot_general x9 -> x0, matrix products: 16.7 us -> none  [the longest x1 6.95 us: expert_ffn(): return jnp.dot(hidden, w_down, preferred_element_type=jnp.float32)]
    unnamed x27 -> x42, local copies, waits for them, and re-layouts: 4.26 us -> 18.6 us
    gather x5 -> x0, local copies, waits for them, and re-layouts: 11.2 us -> none  [the longest x1 3.06 us: on_device(): jnp.take(jnp.concatenate([cache_v, recv_v], axis=0), where_from, axis=0)]
  transfers between devices with their start and end apart: 6 -> 4, of which waited for: 5 -> 4; matrix products, arithmetic and copies ran while one was open for 2% -> 1% of each run, Pallas kernels for 0% -> 0%
where the time goes in v1:
time: 125 us; the launch traced here: 124 us
  waiting for transfers between devices  44.4 us (36%)
  starting transfers between devices  23.2 us (19%)
  Pallas kernels  19.4 us (16%)
  local copies, waits for them, and re-layouts  18.9 us (15%)
  blocking collectives  17.1 us (14%)
    unnamed x42, local copies, waits for them, and re-layouts  18.6 us
    all_to_all x1, blocking collectives, on_device(): lax.all_to_all(rows, ('grp', 'dev'), split_axis=0, concat_axis=0, tiled=T...  17.1 us
    all_to_all x1, waiting for transfers between devices, on_device(): moved = lax.all_to_all(sent, 'grp', split_axis=0, concat_axis=0, tiled=True)  14.2 us
    all_to_all x1, waiting for transfers between devices, on_device(): lax.all_to_all(partial_out, ('grp', 'dev'), split_axis=0, concat_axis=0,...  13.2 us
    all_to_all x1, starting transfers between devices, on_device(): ctx = lax.all_to_all(ctx, 'dev', split_axis=0, concat_axis=0, tiled=True)  9.87 us
    all_to_all x1, waiting for transfers between devices, on_device(): lax.all_to_all(partial_rows, 'dev', split_axis=0, concat_axis=0, tiled=True)  8.63 us
    all_to_all x1, waiting for transfers between devices, on_device(): ctx = lax.all_to_all(ctx, 'dev', split_axis=0, concat_axis=0, tiled=True)  8.43 us
    pallas_call x1, Pallas kernels, on_device(): pl.pallas_call(functools.partial(expert_kernel, groups), name='expert', o...  6.96 us
  transfers between devices with their start and end apart: 4, of which 4 were waited for; matrix products, arithmetic and copies ran while one was open for 1% of the time, Pallas kernels for 0%

profile of v1, /device:TPU:1, one launch (start us, length us, event | category | flops | bytes accessed | tf_op | source)
XLA Modules:
  0.0 124.4 jit_solution(5787512771703135784)
XLA Ops:
  0.7 1.3 %copy-done.4 = bf16[16,8,32,128]{3,2,1,0:T(8,128)(2,1)S(1)} copy-done((bf16[16,8,32,128]{3,2,1,0:T(8,128)(2,1)S(1)}, bf16[16,8,32,128]{3,2,1,0:T(8,128)(2,1)}, u32[]{:S(2)}) %copy-start.4) | copy-done | bytes 1048600
  1.9 1.2 copy-done.6
  3.1 0.7 copy-done.15
  3.8 2.6 %pack.1 = bf16[4,2,2,8,32,128]{5,4,3,2,1,0:T(8,128)(2,1)S(1)} custom-call(s32[64]{0:T(128)S(1)} %copy-done.15, bf16[16,8,32,128]{3,2,1,0:T(8,128)(2,1)S(1)} %copy-done.4, bf16[16,8,32,128]{3,2,1,0:T(8,128)(2,1)S(1)} %copy-done.6), custom_call_target="tpu_custom_call" | custom-call | tf_op jit(solution)/shard_map/pack/pallas_call | solution.py:349
  6.5 1.0 copy-done.8
  7.4 4.8 %all-to-all-start = ((bf16[4,2,2,8,32,128]{5,4,3,2,1,0:T(8,128)(2,1)}), bf16[4,2,2,8,32,128]{5,4,3,2,1,0:T(8,128)(2,1)S(1)}, u32[]{:S(2)}, u32[]{:S(2)}) async-start(bf16[4,2,2,8,32,128]{5,4,3,2,1,0:T(8,128)(2,1)} %copy-done.8), calls=%async_computation | async-start | bytes 2097152 | tf_op jit(solution)/shard_map/all_to_all | solution.py:358
  12.3 14.2 %all-to-all-done.recv = bf16[4,2,2,8,32,128]{5,4,3,2,1,0:T(8,128)(2,1)S(1)} async-done(((bf16[4,2,2,8,32,128]{5,4,3,2,1,0:T(8,128)(2,1)}), bf16[4,2,2,8,32,128]{5,4,3,2,1,0:T(8,128)(2,1)S(1)}, u32[]{:S(2)}, u32[]{:S(2)}) %all-to-all-start) | async-done | bytes 1048608 | tf_op jit(solution)/shard_map/all_to_all | solution.py:358
  26.5 0.8 copy-done.11
  27.2 0.8 copy-done.12
  28.0 0.7 copy-done.16
  28.7 0.7 copy-done.17
  29.3 6.8 %attend.1 = (bf16[16,8,32,128]{3,2,1,0:T(8,128)(2,1)}, bf16[16,8,32,128]{3,2,1,0:T(8,128)(2,1)}, bf16[32,2,16,128]{3,2,1,0:T(8,128)(2,1)S(1)}) custom-call(s32[64]{0:T(128)S(1)} %copy-done.16, s32[16]{0:T(128)S(1)} %copy-done.17, bf16[16,8,32,128]{3,2,1,0:T(8,128)(2,1)S(1)} %copy-done.5, bf16[16,8,32,128]{3,2,1,0:T(8,128)(2,1)S(1)} %copy-done.7, ...), custom_call_target="tpu_custom_call" | custom-call | tf_op jit(solution)/shard_map/attend/pallas_call | solution.py:370
  36.1 0.7 copy-done.10
  36.8 9.9 %all-to-all-start.1 = ((bf16[32,2,16,128]{3,2,1,0:T(8,128)(2,1)}), bf16[32,2,16,128]{3,2,1,0:T(8,128)(2,1)S(1)}, u32[]{:S(2)}, u32[]{:S(2)}) async-start(bf16[32,2,16,128]{3,2,1,0:T(8,128)(2,1)} %copy-done.10), calls=%async_computation.1 | async-start | bytes 524288 | tf_op jit(solution)/shard_map/all_to_all | solution.py:388
  46.8 0.1 eq.15
  46.9 0.2 convert_reduce_fusion
  47.1 8.4 %all-to-all-done.1.recv = bf16[32,2,16,128]{3,2,1,0:T(8,128)(2,1)S(1)} async-done(((bf16[32,2,16,128]{3,2,1,0:T(8,128)(2,1)}), bf16[32,2,16,128]{3,2,1,0:T(8,128)(2,1)S(1)}, u32[]{:S(2)}, u32[]{:S(2)}) %all-to-all-start.1) | async-done | bytes 262176 | tf_op jit(solution)/shard_map/all_to_all | solution.py:388
  55.6 1.7 %copy-done.9 = bf16[192,6144]{1,0:T(8,128)(2,1)S(1)} copy-done((bf16[192,6144]{1,0:T(8,128)(2,1)S(1)}, bf16[192,6144]{1,0:T(8,128)(2,1)}, u32[]{:S(2)}) %copy-start.9) | copy-done | bytes 2359320
  57.2 1.8 %project.1 = bf16[32,2,16,128]{3,2,1,0:T(8,128)(2,1)} custom-call(bf16[32,2,16,128]{3,2,1,0:T(8,128)(2,1)S(1)} %all-to-all-done.1.recv, bf16[192,6144]{1,0:T(8,128)(2,1)S(1)} %copy-done.9), custom_call_target="tpu_custom_call" | custom-call | tf_op jit(solution)/shard_map/project/pallas_call | solution.py:390
  59.1 3.8 %all-to-all-start.2 = ((bf16[32,2,16,128]{3,2,1,0:T(8,128)(2,1)}), bf16[32,2,16,128]{3,2,1,0:T(8,128)(2,1)S(1)}, u32[]{:S(2)}, u32[]{:S(2)}) async-start(bf16[32,2,16,128]{3,2,1,0:T(8,128)(2,1)} %project.1), calls=%async_computation.2 | async-start | bytes 524288 | tf_op jit(solution)/shard_map/all_to_all | solution.py:398
  63.1 8.6 %all-to-all-done.2.recv = bf16[32,2,16,128]{3,2,1,0:T(8,128)(2,1)S(1)} async-done(((bf16[32,2,16,128]{3,2,1,0:T(8,128)(2,1)}), bf16[32,2,16,128]{3,2,1,0:T(8,128)(2,1)S(1)}, u32[]{:S(2)}, u32[]{:S(2)}) %all-to-all-start.2) | async-done | bytes 262176 | tf_op jit(solution)/shard_map/all_to_all | solution.py:398
  71.7 0.7 copy-done.14
  72.4 0.3 dispatch.1
  72.7 17.1 %all_to_all.25.recv = bf16[128,16,128]{2,1,0:T(8,128)(2,1)S(1)} all-to-all(bf16[128,16,128]{2,1,0:T(8,128)(2,1)S(1)} %get-tuple-element.11), channel_id=1, replica_groups=mesh['grp'=4,'dev'=32] {'grp','dev'}, dimensions={0} | all-to-all | bytes 1048576 | tf_op jit(solution)/shard_map/all_to_all | solution.py:411
  89.8 2.8 %copy-done.1 = bf16[6144,512]{1,0:T(8,128)(2,1)S(1)} copy-done((bf16[6144,512]{1,0:T(8,128)(2,1)S(1)}, bf16[6144,512]{1,0:T(8,128)(2,1)}, u32[]{:S(2)}) %copy-start.1) | copy-done | bytes 6291480
  92.6 2.8 %copy-done.2 = bf16[6144,512]{1,0:T(8,128)(2,1)S(1)} copy-done((bf16[6144,512]{1,0:T(8,128)(2,1)S(1)}, bf16[6144,512]{1,0:T(8,128)(2,1)}, u32[]{:S(2)}) %copy-start.2) | copy-done | bytes 6291480
  95.4 2.8 %copy-done.3 = bf16[512,6144]{1,0:T(8,128)(2,1)S(1)} copy-done((bf16[512,6144]{1,0:T(8,128)(2,1)S(1)}, bf16[512,6144]{1,0:T(8,128)(2,1)}, u32[]{:S(2)}) %copy-start.3) | copy-done | bytes 6291480
  98.2 7.0 %expert.1 = bf16[128,16,128]{2,1,0:T(8,128)(2,1)} custom-call(bf16[128,16,128]{2,1,0:T(8,128)(2,1)S(1)} %all_to_all.25.recv, bf16[6144,512]{1,0:T(8,128)(2,1)S(1)} %copy-done.1, bf16[6144,512]{1,0:T(8,128)(2,1)S(1)} %copy-done.2, bf16[512,6144]{1,0:T(8,128)(2,1)S(1)} %copy-done.3), custom_call_target="tpu_custom_call" | custom-call | tf_op jit(solution)/shard_map/expert/pallas_call | solution.py:414
  105.2 4.8 %all-to-all-start.4 = ((bf16[128,16,128]{2,1,0:T(8,128)(2,1)}), bf16[128,16,128]{2,1,0:T(8,128)(2,1)S(1)}, u32[]{:S(2)}, u32[]{:S(2)}) async-start(bf16[128,16,128]{2,1,0:T(8,128)(2,1)} %expert.1), calls=%async_computation.4 | async-start | bytes 1048576 | tf_op jit(solution)/shard_map/all_to_all | solution.py:429
  110.0 0.1 convert_reduce_fusion.1
  110.2 13.2 %all-to-all-done.4.recv = bf16[128,16,128]{2,1,0:T(8,128)(2,1)S(1)} async-done(((bf16[128,16,128]{2,1,0:T(8,128)(2,1)}), bf16[128,16,128]{2,1,0:T(8,128)(2,1)S(1)}, u32[]{:S(2)}, u32[]{:S(2)}) %all-to-all-start.4) | async-done | bytes 524320 | tf_op jit(solution)/shard_map/all_to_all | solution.py:429
  123.4 0.9 final.1
  (36 shorter events, 0.7 us)
Async XLA Ops:
  0.6 11.6 %copy-start = (bf16[16,6144]{1,0:T(8,128)(2,1)S(1)}, bf16[16,6144]{1,0:T(8,128)(2,1)}, u32[]{:S(2)}) copy-start(bf16[16,6144]{1,0:T(8,128)(2,1)} %param.19) | copy-start | bytes 589828
  0.6 1.3 %copy-start.4 = (bf16[16,8,32,128]{3,2,1,0:T(8,128)(2,1)S(1)}, bf16[16,8,32,128]{3,2,1,0:T(8,128)(2,1)}, u32[]{:S(2)}) copy-start(bf16[16,8,32,128]{3,2,1,0:T(8,128)(2,1)} %cache_k.3) | copy-start | bytes 3145732
  1.9 1.2 copy-start.6
  3.1 0.7 copy-start.15
  3.8 22.7 %copy-start.5 = (bf16[16,8,32,128]{3,2,1,0:T(8,128)(2,1)S(1)}, bf16[16,8,32,128]{3,2,1,0:T(8,128)(2,1)}, u32[]{:S(2)}) copy-start(bf16[16,8,32,128]{3,2,1,0:T(8,128)(2,1)} %cache_k.3) | copy-start | bytes 3145732
  3.8 22.7 %copy-start.7 = (bf16[16,8,32,128]{3,2,1,0:T(8,128)(2,1)S(1)}, bf16[16,8,32,128]{3,2,1,0:T(8,128)(2,1)}, u32[]{:S(2)}) copy-start(bf16[16,8,32,128]{3,2,1,0:T(8,128)(2,1)} %cache_v.3) | copy-start | bytes 3145732
  3.8 42.9 %copy-start.18 = (s32[16,2]{0,1:T(2,128)S(1)}, s32[16,2]{0,1:T(2,128)}, u32[]{:S(2)}) copy-start(s32[16,2]{0,1:T(2,128)} %param.28) | copy-start | bytes 388
  3.8 67.9 %copy-start.13 = (bf16[6144]{0:T(1024)(128)(2,1)S(1)}, bf16[6144]{0:T(1024)(128)(2,1)}, u32[]{:S(2)}) copy-start(bf16[6144]{0:T(1024)(128)(2,1)} %param.24) | copy-start | bytes 36868
  6.4 1.0 copy-start.8
  7.4 19.1 %all-to-all-start = ((bf16[4,2,2,8,32,128]{5,4,3,2,1,0:T(8,128)(2,1)}), bf16[4,2,2,8,32,128]{5,4,3,2,1,0:T(8,128)(2,1)S(1)}, u32[]{:S(2)}, u32[]{:S(2)}) async-start(bf16[4,2,2,8,32,128]{5,4,3,2,1,0:T(8,128)(2,1)} %copy-done.8), calls=%async_computation | async-start | bytes 2097152 | tf_op jit(solution)/shard_map/all_to_all | solution.py:358
  26.5 0.8 copy-start.11
  27.2 0.8 copy-start.12
  28.0 0.7 copy-start.16
  28.7 0.7 copy-start.17
  36.1 0.7 copy-start.10
  36.8 18.8 %all-to-all-start.1 = ((bf16[32,2,16,128]{3,2,1,0:T(8,128)(2,1)}), bf16[32,2,16,128]{3,2,1,0:T(8,128)(2,1)S(1)}, u32[]{:S(2)}, u32[]{:S(2)}) async-start(bf16[32,2,16,128]{3,2,1,0:T(8,128)(2,1)} %copy-done.10), calls=%async_computation.1 | async-start | bytes 524288 | tf_op jit(solution)/shard_map/all_to_all | solution.py:388
  55.6 1.7 %copy-start.9 = (bf16[192,6144]{1,0:T(8,128)(2,1)S(1)}, bf16[192,6144]{1,0:T(8,128)(2,1)}, u32[]{:S(2)}) copy-start(bf16[192,6144]{1,0:T(8,128)(2,1)} %weight.1) | copy-start | bytes 7077892
  59.1 12.7 %all-to-all-start.2 = ((bf16[32,2,16,128]{3,2,1,0:T(8,128)(2,1)}), bf16[32,2,16,128]{3,2,1,0:T(8,128)(2,1)S(1)}, u32[]{:S(2)}, u32[]{:S(2)}) async-start(bf16[32,2,16,128]{3,2,1,0:T(8,128)(2,1)} %project.1), calls=%async_computation.2 | async-start | bytes 524288 | tf_op jit(solution)/shard_map/all_to_all | solution.py:398
  71.7 0.7 copy-start.14
  89.8 2.8 %copy-start.1 = (bf16[6144,512]{1,0:T(8,128)(2,1)S(1)}, bf16[6144,512]{1,0:T(8,128)(2,1)}, u32[]{:S(2)}) copy-start(bf16[6144,512]{1,0:T(8,128)(2,1)} %w_gate.1) | copy-start | bytes 18874372
  92.6 2.8 %copy-start.2 = (bf16[6144,512]{1,0:T(8,128)(2,1)S(1)}, bf16[6144,512]{1,0:T(8,128)(2,1)}, u32[]{:S(2)}) copy-start(bf16[6144,512]{1,0:T(8,128)(2,1)} %w_up.1) | copy-start | bytes 18874372
  95.4 2.8 %copy-start.3 = (bf16[512,6144]{1,0:T(8,128)(2,1)S(1)}, bf16[512,6144]{1,0:T(8,128)(2,1)}, u32[]{:S(2)}) copy-start(bf16[512,6144]{1,0:T(8,128)(2,1)} %w_down.1) | copy-start | bytes 18874372
  98.2 11.8 %copy-start.19 = (s32[16,2]{0,1:T(2,128)S(1)}, s32[16,2]{0,1:T(2,128)}, u32[]{:S(2)}) copy-start(s32[16,2]{0,1:T(2,128)} %param.29) | copy-start | bytes 388
  105.2 18.3 %all-to-all-start.4 = ((bf16[128,16,128]{2,1,0:T(8,128)(2,1)}), bf16[128,16,128]{2,1,0:T(8,128)(2,1)S(1)}, u32[]{:S(2)}, u32[]{:S(2)}) async-start(bf16[128,16,128]{2,1,0:T(8,128)(2,1)} %expert.1), calls=%async_computation.4 | async-start | bytes 1048576 | tf_op jit(solution)/shard_map/all_to_all | solution.py:429

commit v2 on v1

v2 whole, which is shorter than its diff:
```python
import functools

import jax
import jax.numpy as jnp
from jax import lax
from jax.experimental import pallas as pl
from jax.experimental.pallas import tpu as pltpu
from jax.sharding import PartitionSpec as P

EXPERTS = 8
MOVE = 2
CAP = 8
LANES = 128
HALF = 64
F32 = jnp.float32
BF16 = jnp.bfloat16
VMEM = pl.BlockSpec(memory_space=pltpu.VMEM)
SMEM = pl.BlockSpec(memory_space=pltpu.SMEM)
HBM = pl.BlockSpec(memory_space=pltpu.HBM)


def pieces(value, count):
    terms = []
    for _ in range(count):
        term = value.astype(BF16).astype(F32)
        terms.append(term)
        value = value - term
    return terms


def iota(shape, dim):
    return lax.broadcasted_iota(jnp.int32, shape, dim)


def places(value, size):
    bits = size.bit_length() - 1
    assert size == 1 << bits
    return value >> bits, value & (size - 1)


def pack_kernel(groups, per, source, cache_k, cache_v, out, src, buf, src_sem, in_sem, out_sem):
    pltpu.make_async_copy(source, src, src_sem).start()
    me = lax.axis_index("grp")
    pltpu.make_async_copy(source, src, src_sem).wait()
    loads, stores = [], []
    for dest in range(groups):
        count = jnp.int32(0)
        picks = [jnp.int32(0)] * MOVE
        for slot in range(per):
            owner, old = places(src[dest * per + slot], per)
            mine = (owner == me) & (me != dest)
            for rank in range(MOVE):
                picks[rank] = jnp.where(mine & (count == rank), old, picks[rank])
            count = count + mine.astype(jnp.int32)
        for rank in range(MOVE):
            for which, cache in ((0, cache_k), (1, cache_v)):
                copy = pltpu.make_async_copy(
                    cache.at[picks[rank]], buf.at[dest, which, rank], in_sem.at[dest, which, rank]
                )
                copy.start()
                loads.append((copy, dest, which, rank))
    for load, dest, which, rank in loads:
        load.wait()
        copy = pltpu.make_async_copy(
            buf.at[dest, which, rank], out.at[dest, which, rank], out_sem.at[dest, which, rank]
        )
        copy.start()
        stores.append(copy)
    for copy in stores:
        copy.wait()


def column(values):
    rows = iota((len(values), 1), 0)
    result = jnp.zeros((len(values), 1), jnp.int32)
    for at, value in enumerate(values):
        result = jnp.where(rows == at, value, result)
    return result


def stay_kernel(
    groups, per, source, lengths, cache_k, cache_v, query, new_key, new_value, resid, gain,
    spare_valid, peaks, totals, contexts, start, gains, kbuf, vbuf, src, length, sems,
):
    copies = [
        pltpu.make_async_copy(a, b, sems.at[j])
        for j, (a, b) in enumerate(
            ((source, src), (lengths, length), (cache_k, kbuf), (cache_v, vbuf))
        )
    ]
    for copy in copies:
        copy.start()
    me = lax.axis_index("grp")
    heads_kv, block = kbuf.shape[1], kbuf.shape[2]
    share = query.shape[0] // heads_kv
    base = lax.axis_index("dev") * block
    copies[0].wait()
    copies[1].wait()
    counts = [jnp.int32(0)] * groups
    spots, limits, arrivals = [], [], []
    for slot in range(per):
        owner = places(src[me * per + slot], per)[0]
        rank = jnp.int32(0)
        for g in range(groups):
            here = owner == g
            rank = jnp.where(here, counts[g], rank)
            counts[g] = counts[g] + here.astype(jnp.int32)
        spot = length[slot] - base
        spots.append(spot)
        limits.append(jnp.where(owner == me, spot, -1))
        arrivals.append(jnp.where(owner == me, -1, owner * MOVE + rank))
    spot, limit, arrival = column(spots), column(limits), column(arrivals)
    which, where = places(iota((per, per * block), 1), block)
    valid = (which == iota((per, per * block), 0)) & (where < limit)
    which, where = places(iota((per, groups * MOVE * block), 1), block)
    spare_valid[...] = ((which == arrival) & (where < spot)).astype(F32)
    fresh = (spot >= 0) & (spot < block)
    copies[2].wait()
    copies[3].wait()
    scale = LANES**-0.5
    for kv in range(heads_kv):
        keys = kbuf[:, kv].reshape(per * block, LANES)
        values = vbuf[:, kv].reshape(per * block, LANES)
        rows = query[kv * share : (kv + 1) * share]
        scores = lax.dot_general(
            rows.reshape(share * per, LANES), keys, (((1,), (1,)), ((), ())),
            preferred_element_type=F32,
        ).reshape(share, per, per * block) * scale
        scores = jnp.where(valid[None], scores, F32(-1e30))
        newest = jnp.sum(
            rows.astype(F32) * new_key[kv].astype(F32)[None], axis=-1, keepdims=True
        ) * scale
        newest = jnp.where(fresh[None], newest, F32(-1e30))
        peak = jnp.maximum(jnp.max(scores, axis=-1, keepdims=True), newest)
        weights = jnp.where(valid[None], jnp.exp(scores - peak), F32(0.0)).astype(BF16)
        added = jnp.where(fresh[None], jnp.exp(newest - peak), F32(0.0))
        total = jnp.sum(weights.astype(F32), axis=-1, keepdims=True) + added
        context = jnp.dot(
            weights.reshape(share * per, per * block), values, preferred_element_type=F32
        ).reshape(share, per, LANES) + added * new_value[kv].astype(F32)[None]
        at = slice(kv * share, (kv + 1) * share)
        peaks[at] = jnp.broadcast_to(peak, (share, per, LANES))
        totals[at] = jnp.broadcast_to(total, (share, per, LANES))
        contexts[at] = context
    dev = lax.axis_index("dev")
    even = dev % 2 == 0
    tiles = tiles_of(even, resid[...].astype(F32))
    lane = iota((1, LANES), 1)
    spare = (jnp.logical_not(even) & (lane < HALF), even & (lane >= HALF))
    for k in range(2):
        start[k] = tiles[k]
        at = 3 * (dev // 2) + dev % 2 + k
        own = jnp.where(iota(gain.shape, 0) == at, gain[...].astype(F32), F32(0.0))
        gains[k : k + 1] = jnp.where(spare[k], F32(0.0), jnp.sum(own, axis=0, keepdims=True))


def arrive_kernel(moved, query, spare_valid, peaks, totals, contexts, out, buf, sems):
    groups, _, _, heads_kv, block, _ = moved.shape
    share, per = query.shape[0] // heads_kv, query.shape[1]
    columns = groups * MOVE * block
    valid = spare_valid[...] > 0.5
    scale = LANES**-0.5
    ones = jnp.ones((columns, LANES), BF16)
    lane = iota((1, 1, LANES), 2)
    lane2 = iota((per, LANES), 1)
    first = ((lane2 >> 3) & 1) == 0
    low = lane2 < HALF
    copies = []
    for kv in range(heads_kv):
        keys = moved[:, 0, :, kv].reshape(columns, LANES)
        values = moved[:, 1, :, kv].reshape(columns, LANES)
        at = slice(kv * share, (kv + 1) * share)
        scores = lax.dot_general(
            query[at].reshape(share * per, LANES), keys, (((1,), (1,)), ((), ())),
            preferred_element_type=F32,
        ).reshape(share, per, columns) * scale
        scores = jnp.where(valid[None], scores, F32(-1e30))
        before = peaks[at]
        peak = jnp.maximum(before, jnp.max(scores, axis=-1, keepdims=True))
        whole = jnp.concatenate([peak] * (columns // LANES), axis=-1)
        weights = jnp.where(valid[None], jnp.exp(scores - whole), F32(0.0)).astype(BF16)
        keep = jnp.exp(before - peak)
        sums = jnp.dot(
            weights.reshape(share * per, columns),
            jnp.concatenate([values, ones], axis=1),
            preferred_element_type=F32,
        ).reshape(share, per, 2 * LANES)
        context = sums[..., :LANES] + keep * contexts[at]
        total = sums[..., LANES:] + keep * totals[at]
        stat = jnp.zeros((share, per, LANES), F32)
        for j, term in enumerate(pieces(peak, 3) + pieces(total, 2)):
            stat = jnp.where((lane & 7) == j, term, stat)
        for i in range(share // 3):
            m = kv * (share // 3) + i
            a, b, c = (context[3 * i + j] for j in range(3))
            sa, sb, sc = (stat[3 * i + j] for j in range(3))
            buf[2 * m, 0] = a.astype(BF16)
            buf[2 * m, 1] = jnp.where(low, b, jnp.where(first, sa, sb)).astype(BF16)
            buf[2 * m + 1, 0] = jnp.where(low, jnp.where(first, sb, sc), b).astype(BF16)
            buf[2 * m + 1, 1] = c.astype(BF16)
        part = pl.ds(2 * kv * (share // 3), 2 * (share // 3))
        copy = pltpu.make_async_copy(buf.at[part], out.at[part], sems.at[kv])
        copy.start()
        copies.append(copy)
    for copy in copies:
        copy.wait()


def store_kernel(
    groups, per, source, lengths, cache_k, cache_v, moved, new_key, new_value,
    out_k, out_v, kbuf, vbuf, src, length, small_sem, in_sem, out_sem,
):
    small = [
        pltpu.make_async_copy(source, src, small_sem.at[0]),
        pltpu.make_async_copy(lengths, length, small_sem.at[1]),
    ]
    for copy in small:
        copy.start()
    me = lax.axis_index("grp")
    heads_kv, block = kbuf.shape[1], kbuf.shape[2]
    base = lax.axis_index("dev") * block
    for copy in small:
        copy.wait()
    counts = [jnp.int32(0)] * groups
    for slot in range(per):
        owner = places(src[me * per + slot], per)[0]
        stays = owner == me
        rank = jnp.int32(0)
        for g in range(groups):
            here = owner == g
            rank = jnp.where(here, counts[g], rank)
            counts[g] = counts[g] + here.astype(jnp.int32)
        rank = jnp.minimum(rank, MOVE - 1)

        @pl.when(stays)
        def _():
            pltpu.make_async_copy(cache_k.at[slot], kbuf.at[slot], in_sem.at[0, slot]).start()
            pltpu.make_async_copy(cache_v.at[slot], vbuf.at[slot], in_sem.at[1, slot]).start()

        @pl.when(jnp.logical_not(stays))
        def _():
            pltpu.make_async_copy(moved.at[owner, 0, rank], kbuf.at[slot], in_sem.at[0, slot]).start()
            pltpu.make_async_copy(moved.at[owner, 1, rank], vbuf.at[slot], in_sem.at[1, slot]).start()

    outs = []
    for slot in range(per):
        pltpu.make_async_copy(cache_k.at[0], kbuf.at[slot], in_sem.at[0, slot]).wait()
        pltpu.make_async_copy(cache_v.at[0], vbuf.at[slot], in_sem.at[1, slot]).wait()
        spot = length[slot] - base

        @pl.when((spot >= 0) & (spot < block))
        def _():
            hit = iota((heads_kv, block, LANES), 1) == spot
            kbuf[slot] = jnp.where(hit, new_key[slot][:, None, :], kbuf[slot])
            vbuf[slot] = jnp.where(hit, new_value[slot][:, None, :], vbuf[slot])

        for which, buf, out in ((0, kbuf, out_k), (1, vbuf, out_v)):
            copy = pltpu.make_async_copy(buf.at[slot], out.at[slot], out_sem.at[which, slot])
            copy.start()
            outs.append(copy)
    for copy in outs:
        copy.wait()


def project_kernel(recv, weight, out, wbuf, buf, w_sems, sems):
    span = wbuf.shape[2]
    loads = []
    for j in range(wbuf.shape[0]):
        copy = pltpu.make_async_copy(
            weight.at[:, pl.ds(j * span, span)], wbuf.at[j], w_sems.at[j]
        )
        copy.start()
        loads.append(copy)
    even = lax.axis_index("dev") % 2 == 0
    per = recv.shape[2]
    peers = recv.shape[0]
    stat = jnp.where(even, recv[:, 1], recv[:, 0]).reshape(peers * per, LANES)
    kind, _ = places(iota((LANES, 4 * LANES), 1), LANES)
    term = iota((LANES, 4 * LANES), 0) - jnp.where(even, HALF, 0) - 8 * (kind >> 1)
    begin = 3 * (kind & 1)
    wanted = (term >= begin) & (term < 3 + 2 * (kind & 1))
    spread = jnp.dot(
        stat, wanted.astype(F32).astype(BF16), preferred_element_type=F32
    ).reshape(peers, per, 4 * LANES)
    parts = []
    for k in range(2):
        peak = spread[..., 2 * k * LANES : (2 * k + 1) * LANES]
        total = spread[..., (2 * k + 1) * LANES : (2 * k + 2) * LANES]
        factor = jnp.exp(peak - jnp.max(peak, axis=0, keepdims=True))
        whole = jnp.sum(factor * total, axis=0)
        parts.append(jnp.sum(factor * recv[:, k].astype(F32), axis=0) / whole)
    both = jnp.concatenate(parts, axis=1)
    rows = weight.shape[0]
    attn = jnp.where(even, both[:, :rows], both[:, 2 * LANES - rows :]).astype(BF16)
    copies = []
    for m in range(out.shape[0] // 2):
        j, at = divmod(3 * LANES * m, span)
        if at == 0:
            loads[j].wait()
        part = jnp.dot(
            attn, wbuf[j, :, at : at + 3 * LANES], preferred_element_type=F32
        ).astype(BF16)
        t0, t1, t2 = (part[:, LANES * j : LANES * (j + 1)] for j in range(3))
        buf[2 * m, 0] = t0
        buf[2 * m, 1] = t1
        buf[2 * m + 1, 0] = t1
        buf[2 * m + 1, 1] = t2
        part = pl.ds(2 * m, 2)
        copy = pltpu.make_async_copy(buf.at[part], out.at[part], sems.at[m])
        copy.start()
        copies.append(copy)
    for copy in copies:
        copy.wait()


def tiles_of(even, wide):
    rows = wide.shape[0]
    zero = jnp.zeros((rows, HALF), wide.dtype)
    left = jnp.concatenate([wide, zero], axis=1)
    right = jnp.concatenate([zero, wide], axis=1)
    both = jnp.where(even, left, right)
    return both[:, :LANES], both[:, LANES:]


def dispatch_kernel(recv, start, gains, qrow, mixed, out):
    even = lax.axis_index("dev") % 2 == 0
    per = recv.shape[2]
    lane = iota((per, LANES), 1)
    spare = (jnp.logical_not(even) & (lane < HALF), even & (lane >= HALF))
    square = jnp.zeros((per, 1), F32)
    wides = []
    for k in range(2):
        part = start[k] + jnp.sum(recv[:, k].astype(F32), axis=0)
        part = jnp.where(spare[k], F32(0.0), part)
        mixed[k] = part
        square = square + jnp.sum(part * part, axis=1, keepdims=True)
        wides.append(part * gains[k : k + 1])
    stat = jnp.zeros((per, LANES), F32)
    for at, term in enumerate(pieces(square, 3)):
        stat = jnp.where((lane & 7) == at, term, stat)
    rows = jnp.concatenate(
        [jnp.where(spare[k], stat, wides[k]).astype(BF16) for k in range(2)], axis=0
    )
    count = EXPERTS * 2 * CAP
    where = iota((count, 2 * per), 0)
    from_ = iota((count, 2 * per), 1)
    expert, _ = places(where, 2 * CAP)
    half, place = places(where, CAP)
    slot = expert * CAP + place
    named = (slot == qrow[0:1, :]) | (slot == qrow[1:2, :])
    pick = (named & ((half & 1) == places(from_, per)[0])).astype(F32).astype(BF16)
    sent = jnp.dot(pick, rows, preferred_element_type=F32).astype(BF16)
    split = out.shape[0] // EXPERTS
    for e in range(EXPERTS):
        block = sent[2 * CAP * e : 2 * CAP * (e + 1)]
        for s in range(split):
            out[e * split + s] = block


def expert_kernel(groups, recv, w_gate, w_up, w_down, out, xbuf, buf, wg, wu, wd, w_sems, sems):
    width = xbuf.shape[1]
    depth, span = wg.shape[1], wd.shape[2]
    firsts, seconds = [], []
    for j in range(wg.shape[0]):
        rows = pl.ds(j * depth, depth)
        pair = (
            pltpu.make_async_copy(w_gate.at[rows], wg.at[j], w_sems.at[0, j]),
            pltpu.make_async_copy(w_up.at[rows], wu.at[j], w_sems.at[1, j]),
        )
        for copy in pair:
            copy.start()
        firsts.append(pair)
    for j in range(wd.shape[0]):
        copy = pltpu.make_async_copy(
            w_down.at[:, pl.ds(j * span, span)], wd.at[j], w_sems.at[2, j]
        )
        copy.start()
        seconds.append(copy)
    devs = recv.shape[0] // groups
    lane = iota((CAP, LANES), 1)
    low = lane < HALF
    rows_square = []
    for g in range(groups):
        acc = jnp.zeros((CAP, LANES), F32)
        for m in range(devs // 2):
            e, o = recv[g * devs + 2 * m], recv[g * devs + 2 * m + 1]
            middle_e, middle_o = e[CAP:].astype(F32), o[:CAP].astype(F32)
            acc = acc + jnp.where(low, middle_o, middle_e)
            at = slice(CAP * g, CAP * (g + 1))
            xbuf[at, 3 * LANES * m : 3 * LANES * m + LANES] = e[:CAP]
            xbuf[at, 3 * LANES * m + LANES : 3 * LANES * m + 2 * LANES] = jnp.where(
                low, middle_e, middle_o
            ).astype(BF16)
            xbuf[at, 3 * LANES * m + 2 * LANES : 3 * LANES * (m + 1)] = o[CAP:]
        both = acc[:, :8] + acc[:, HALF : HALF + 8]
        rows_square.append(both[:, 0:1] + both[:, 1:2] + both[:, 2:3])
    square = jnp.concatenate(rows_square, axis=0)
    scale = lax.rsqrt(square / width + 1e-05)
    gate = jnp.zeros((groups * CAP, wg.shape[2]), F32)
    up = jnp.zeros((groups * CAP, wu.shape[2]), F32)
    for j, pair in enumerate(firsts):
        x = xbuf[:, depth * j : depth * (j + 1)]
        pair[0].wait()
        gate = gate + jnp.dot(x, wg[j], preferred_element_type=F32)
        pair[1].wait()
        up = up + jnp.dot(x, wu[j], preferred_element_type=F32)
    gate, up = gate * scale, up * scale
    hidden = (gate / (1.0 + jnp.exp(-gate)) * up).astype(BF16)
    copies = []
    for m in range(devs // 2):
        j, at = divmod(3 * LANES * m, span)
        if at == 0:
            seconds[j].wait()
        part = jnp.dot(
            hidden, wd[j, :, at : at + 3 * LANES], preferred_element_type=F32
        )
        t = [part[:, LANES * k : LANES * (k + 1)] for k in range(3)]
        for g in range(groups):
            at = slice(CAP * g, CAP * (g + 1))
            for i in range(2):
                buf[g, 2 * m + i] = jnp.concatenate([t[i][at], t[i + 1][at]], axis=0).astype(BF16)
            copy = pltpu.make_async_copy(
                buf.at[g, pl.ds(2 * m, 2)], out.at[pl.ds(g * devs + 2 * m, 2)], sems.at[g, m]
            )
            copy.start()
            copies.append(copy)
    for copy in copies:
        copy.wait()


def final_kernel(recv, mixed, qcol, share, out):
    even = lax.axis_index("dev") % 2 == 0
    split = recv.shape[0] // EXPERTS
    per = mixed.shape[1]
    sums = [
        jnp.sum(recv[e * split : (e + 1) * split].astype(F32), axis=0) for e in range(EXPERTS)
    ]
    slot = iota((per, EXPERTS * CAP), 1)
    weight = jnp.where(slot == qcol[:, 0:1], share[:, 0:1], F32(0.0)) + jnp.where(
        slot == qcol[:, 1:2], share[:, 1:2], F32(0.0)
    )
    done = []
    for k in range(2):
        expert = jnp.concatenate([s[CAP * k : CAP * (k + 1)] for s in sums], axis=0)
        moe = jnp.dot(
            weight, expert, preferred_element_type=F32, precision=lax.Precision.HIGHEST
        )
        done.append(mixed[k] + moe)
    both = jnp.concatenate(done, axis=1)
    width = out.shape[1]
    out[...] = jnp.where(even, both[:, :width], both[:, 2 * LANES - width :]).astype(BF16)


def params(free):
    return pltpu.CompilerParams(vmem_limit_bytes=67043328 - free)


def on_device(
    cache_k,
    cache_v,
    source,
    lengths,
    query,
    new_key,
    new_value,
    resid,
    out_weight,
    norm_gain,
    w_gate,
    w_up,
    w_down,
    expert_ids,
    gate_codes,
):
    groups = lax.axis_size("grp")
    devs = lax.axis_size("dev")
    per, kv_heads, block, head_dim = cache_k.shape
    heads = query.shape[1] // head_dim
    width = query.shape[1]
    hidden = w_gate.shape[1]
    sds = jax.ShapeDtypeStruct
    cache_k, cache_v, source, lengths, out_weight, w_gate, w_up, w_down = (
        pltpu.with_memory_space_constraint(a, pltpu.HBM)
        for a in (cache_k, cache_v, source, lengths, out_weight, w_gate, w_up, w_down)
    )
    move_shape = (groups, 2, MOVE, kv_heads, block, head_dim)

    sent = pl.pallas_call(
        functools.partial(pack_kernel, groups, per),
        name="pack",
        out_shape=sds(move_shape, BF16),
        in_specs=[HBM, HBM, HBM],
        out_specs=HBM,
        scratch_shapes=[
            pltpu.SMEM(source.shape, jnp.int32),
            pltpu.VMEM(move_shape, BF16),
            pltpu.SemaphoreType.DMA,
            pltpu.SemaphoreType.DMA((groups, 2, MOVE)),
            pltpu.SemaphoreType.DMA((groups, 2, MOVE)),
        ],
        compiler_params=params(56 << 20),
    )(source, cache_k, cache_v)
    moved = lax.all_to_all(sent, "grp", split_axis=0, concat_axis=0, tiled=True)

    flat = expert_ids.reshape(-1)
    order = jnp.arange(flat.shape[0], dtype=jnp.int32)
    same = (flat[:, None] == flat[None, :]) & (order[None, :] < order[:, None])
    qflat = flat * CAP + jnp.sum(same.astype(jnp.int32), axis=1)
    qcol = qflat.reshape(per, 2)
    qrow = jnp.concatenate([qcol.T, qcol.T], axis=1)
    codes = gate_codes.astype(F32)
    share = codes / jnp.sum(codes, axis=-1, keepdims=True)
    by_head = query.reshape(per, heads, head_dim).transpose(1, 0, 2)

    row_shape = sds((heads, per, LANES), F32)
    spare_valid, peaks, totals, contexts, start, gains = pl.pallas_call(
        functools.partial(stay_kernel, groups, per),
        name="stay",
        out_shape=(
            sds((per, groups * MOVE * block), F32),
            row_shape,
            row_shape,
            row_shape,
            sds((2, per, LANES), F32),
            sds((2, LANES), F32),
        ),
        in_specs=[HBM, HBM, HBM, HBM, VMEM, VMEM, VMEM, VMEM, VMEM],
        out_specs=(VMEM,) * 6,
        scratch_shapes=[
            pltpu.VMEM(cache_k.shape, BF16),
            pltpu.VMEM(cache_v.shape, BF16),
            pltpu.SMEM(source.shape, jnp.int32),
            pltpu.SMEM(lengths.shape, jnp.int32),
            pltpu.SemaphoreType.DMA((4,)),
        ],
        compiler_params=params(48 << 20),
        cost_estimate=pl.CostEstimate(flops=0, transcendentals=0, bytes_accessed=16 << 20),
    )(
        source, lengths, cache_k, cache_v, by_head,
        new_key.transpose(1, 0, 2), new_value.transpose(1, 0, 2), resid,
        norm_gain.reshape(-1, LANES),
    )

    ctx = pl.pallas_call(
        arrive_kernel,
        name="arrive",
        out_shape=sds((devs, 2, per, LANES), BF16),
        in_specs=[VMEM] * 6,
        out_specs=HBM,
        scratch_shapes=[
            pltpu.VMEM((devs, 2, per, LANES), BF16),
            pltpu.SemaphoreType.DMA((kv_heads,)),
        ],
        compiler_params=params(52 << 20),
    )(moved, by_head, spare_valid, peaks, totals, contexts)
    ctx = lax.all_to_all(ctx, "dev", split_axis=0, concat_axis=0, tiled=True)

    new_k, new_v = pl.pallas_call(
        functools.partial(store_kernel, groups, per),
        name="store",
        out_shape=(sds(cache_k.shape, BF16), sds(cache_v.shape, BF16)),
        in_specs=[HBM, HBM, HBM, HBM, pl.BlockSpec(memory_space=pl.ANY), VMEM, VMEM],
        out_specs=(HBM, HBM),
        scratch_shapes=[
            pltpu.VMEM(cache_k.shape, BF16),
            pltpu.VMEM(cache_v.shape, BF16),
            pltpu.SMEM(source.shape, jnp.int32),
            pltpu.SMEM(lengths.shape, jnp.int32),
            pltpu.SemaphoreType.DMA((2,)),
            pltpu.SemaphoreType.DMA((2, per)),
            pltpu.SemaphoreType.DMA((2, per)),
        ],
        compiler_params=params(52 << 20),
        cost_estimate=pl.CostEstimate(flops=0, transcendentals=0, bytes_accessed=8 << 20),
    )(source, lengths, cache_k, cache_v, moved, new_key, new_value)

    partial_rows = pl.pallas_call(
        project_kernel,
        name="project",
        out_shape=sds((devs, 2, per, LANES), BF16),
        in_specs=[VMEM, HBM],
        out_specs=HBM,
        scratch_shapes=[
            pltpu.VMEM((8, out_weight.shape[0], width // 8), BF16),
            pltpu.VMEM((devs, 2, per, LANES), BF16),
            pltpu.SemaphoreType.DMA((8,)),
            pltpu.SemaphoreType.DMA((devs // 2,)),
        ],
        compiler_params=params(52 << 20),
    )(ctx, out_weight)
    partial_rows = lax.all_to_all(partial_rows, "dev", split_axis=0, concat_axis=0, tiled=True)

    mixed, rows = pl.pallas_call(
        dispatch_kernel,
        name="dispatch",
        out_shape=(
            sds((2, per, LANES), F32),
            sds((groups * devs, 2 * CAP, LANES), BF16),
        ),
        in_specs=[VMEM] * 4,
        out_specs=(VMEM, VMEM),
        compiler_params=params(56 << 20),
    )(partial_rows, start, gains, qrow)
    rows = lax.all_to_all(rows, ("grp", "dev"), split_axis=0, concat_axis=0, tiled=True)

    chunks, down_chunks = 12, 8
    partial_out = pl.pallas_call(
        functools.partial(expert_kernel, groups),
        name="expert",
        out_shape=sds((groups * devs, 2 * CAP, LANES), BF16),
        in_specs=[VMEM, HBM, HBM, HBM],
        out_specs=HBM,
        scratch_shapes=[
            pltpu.VMEM((groups * CAP, width), BF16),
            pltpu.VMEM((groups, devs, 2 * CAP, LANES), BF16),
            pltpu.VMEM((chunks, width // chunks, hidden), BF16),
            pltpu.VMEM((chunks, width // chunks, hidden), BF16),
            pltpu.VMEM((down_chunks, hidden, width // down_chunks), BF16),
            pltpu.SemaphoreType.DMA((3, chunks)),
            pltpu.SemaphoreType.DMA((groups, devs // 2)),
        ],
        compiler_params=params(32 << 20),
    )(rows, w_gate, w_up, w_down)
    partial_out = lax.all_to_all(
        partial_out, ("grp", "dev"), split_axis=0, concat_axis=0, tiled=True
    )

    layer_out = pl.pallas_call(
        final_kernel,
        name="final",
        out_shape=sds(resid.shape, BF16),
        in_specs=[VMEM] * 4,
        out_specs=VMEM,
        compiler_params=params(56 << 20),
    )(partial_out, mixed, qcol, share)
    return (new_k, new_v, layer_out)


def solution(mesh):
    in_specs = (
        P("grp", None, "dev", None),
        P("grp", None, "dev", None),
        P(),
        P("grp"),
        P("grp", None),
        P("grp", None, None),
        P("grp", None, None),
        P("grp", "dev"),
        P("dev", None),
        P(),
        P(None, ("grp", "dev")),
        P(None, ("grp", "dev")),
        P(("grp", "dev"), None),
        P("grp", None),
        P("grp", None),
    )
    out_specs = (P("grp", None, "dev", None), P("grp", None, "dev", None), P("grp", "dev"))
    return jax.shard_map(
        on_device, mesh=mesh, in_specs=in_specs, out_specs=out_specs, check_vma=False
    )
```

time: 125 us -> 107 us (0.86)
  waiting for transfers between devices: 44.4 us -> 25.5 us
  blocking collectives: 17.1 us -> 35.7 us
  local copies, waits for them, and re-layouts: 18.9 us -> 2.74 us
  starting transfers between devices: 23.2 us -> 13.6 us
  Pallas kernels: 19.4 us -> 27 us
    all_to_all x0 -> x1, blocking collectives: none -> 18.6 us  [on_device(): ctx = lax.all_to_all(ctx, 'dev', split_axis=0, concat_axis=0, tiled=True)]
    unnamed x42 -> x16, local copies, waits for them, and re-layouts: 18.6 us -> 1.59 us
    all_to_all x1 -> x0, starting transfers between devices: 9.87 us -> none  [on_device(): ctx = lax.all_to_all(ctx, 'dev', split_axis=0, concat_axis=0, tiled=True)]
    all_to_all x1 -> x0, waiting for transfers between devices: 8.43 us -> none  [on_device(): ctx = lax.all_to_all(ctx, 'dev', split_axis=0, concat_axis=0, tiled=True)]
    all_to_all x1, waiting for transfers between devices: 14.2 us -> 8.18 us  [on_device(): moved = lax.all_to_all(sent, 'grp', split_axis=0, concat_axis=0, tiled=True)]
    pallas_call x1 -> x3, Pallas kernels: 6.76 us -> 11.3 us  [the longest x1 4 us: on_device(): pl.pallas_call(functools.partial(store_kernel, groups, per), name='store'...]
    all_to_all x1, waiting for transfers between devices: 13.2 us -> 9.17 us  [on_device(): lax.all_to_all(partial_out, ('grp', 'dev'), split_axis=0, concat_axis=0,...]
    pallas_call x1, Pallas kernels: 6.96 us -> 8.27 us  [on_device(): pl.pallas_call(functools.partial(expert_kernel, groups), name='expert', o...]
  transfers between devices with their start and end apart: 4 -> 3, of which waited for: 4 -> 3; matrix products, arithmetic and copies ran while one was open for 1% -> 2% of each run, Pallas kernels for 0% -> 7%
where the time goes in v2:
time: 107 us; the launch traced here: 106 us
  blocking collectives  35.7 us (33%)
  Pallas kernels  27 us (25%)
  waiting for transfers between devices  25.5 us (24%)
  starting transfers between devices  13.6 us (13%)
  local copies, waits for them, and re-layouts  2.74 us (3%)
    all_to_all x1, blocking collectives, on_device(): ctx = lax.all_to_all(ctx, 'dev', split_axis=0, concat_axis=0, tiled=True)  18.6 us
    all_to_all x1, blocking collectives, on_device(): lax.all_to_all(rows, ('grp', 'dev'), split_axis=0, concat_axis=0, tiled=T...  17.1 us
    all_to_all x1, waiting for transfers between devices, on_device(): lax.all_to_all(partial_out, ('grp', 'dev'), split_axis=0, concat_axis=0,...  9.17 us
    pallas_call x1, Pallas kernels, on_device(): pl.pallas_call(functools.partial(expert_kernel, groups), name='expert', o...  8.27 us
    all_to_all x1, waiting for transfers between devices, on_device(): moved = lax.all_to_all(sent, 'grp', split_axis=0, concat_axis=0, tiled=True)  8.18 us
    all_to_all x1, waiting for transfers between devices, on_device(): lax.all_to_all(partial_rows, 'dev', split_axis=0, concat_axis=0, tiled=True)  8.18 us
    all_to_all x1, starting transfers between devices, on_device(): moved = lax.all_to_all(sent, 'grp', split_axis=0, concat_axis=0, tiled=True)  5.08 us
    all_to_all x1, starting transfers between devices, on_device(): lax.all_to_all(partial_out, ('grp', 'dev'), split_axis=0, concat_axis=0,...  4.78 us
  transfers between devices with their start and end apart: 3, of which 3 were waited for; matrix products, arithmetic and copies ran while one was open for 2% of the time, Pallas kernels for 7%

profile of v2, /device:TPU:1, one launch (start us, length us, event | category | flops | bytes accessed | tf_op | source)
XLA Modules:
  0.0 105.8 jit_solution(7934678623597197781)
XLA Ops:
  0.6 0.0 copy-start
  0.6 3.1 %pack.1 = bf16[4,2,2,8,32,128]{5,4,3,2,1,0:T(8,128)(2,1)} custom-call(s32[64]{0:T(128)} %source.5, bf16[16,8,32,128]{3,2,1,0:T(8,128)(2,1)} %cache_k.5, bf16[16,8,32,128]{3,2,1,0:T(8,128)(2,1)} %cache_v.5), custom_call_target="tpu_custom_call" | custom-call | tf_op jit(solution)/shard_map/pack/pallas_call | solution.py:488
  3.7 0.0 copy-start.5
  3.8 5.1 %all-to-all-start = ((bf16[4,2,2,8,32,128]{5,4,3,2,1,0:T(8,128)(2,1)}), bf16[4,2,2,8,32,128]{5,4,3,2,1,0:T(8,128)(2,1)S(1)}, u32[]{:S(2)}, u32[]{:S(2)}) async-start(bf16[4,2,2,8,32,128]{5,4,3,2,1,0:T(8,128)(2,1)} %pack.1), calls=%async_computation | async-start | bytes 2097152 | tf_op jit(solution)/shard_map/all_to_all | solution.py:503
  8.8 0.8 copy_bitcast_fusion
  9.7 0.0 copy-start.3
  9.7 0.7 copy-done.3
  10.4 0.7 copy-done.4
  11.1 3.8 %stay.1 = (f32[16,256]{1,0:T(8,128)S(1)}, f32[48,16,128]{2,1,0:T(8,128)S(1)}, f32[48,16,128]{2,1,0:T(8,128)S(1)}, f32[48,16,128]{2,1,0:T(8,128)S(1)}, f32[2,16,128]{2,1,0:T(8,128)S(1)}, /*index=5*/f32[2,128]{1,0:T(2,128)S(1)}) custom-call(s32[64]{0:T(128)} %source.5, s32[16]{0:T(128)} %lengths.3, bf16[16,8,32,128]{3,2,1,0:T(8,128)(2,1)} %cache_k.5, ...), custom_call_target="tpu_custom_call" | custom-call | bytes 16777216 | tf_op jit(solution)/shard_map/stay/pallas_call | solution.py:516
  14.9 8.2 %all-to-all-done.moved = bf16[4,2,2,8,32,128]{5,4,3,2,1,0:T(8,128)(2,1)S(1)} async-done(((bf16[4,2,2,8,32,128]{5,4,3,2,1,0:T(8,128)(2,1)}), bf16[4,2,2,8,32,128]{5,4,3,2,1,0:T(8,128)(2,1)S(1)}, u32[]{:S(2)}, u32[]{:S(2)}) %all-to-all-start) | async-done | bytes 1048608 | tf_op jit(solution)/shard_map/all_to_all | solution.py:503
  23.1 3.5 %arrive.1 = bf16[32,2,16,128]{3,2,1,0:T(8,128)(2,1)S(1)} custom-call(bf16[4,2,2,8,32,128]{5,4,3,2,1,0:T(8,128)(2,1)S(1)} %all-to-all-done.moved, bf16[48,16,128]{2,1,0:T(8,128)(2,1)S(1)} %bitcast_bitcast_fusion.query, f32[16,256]{1,0:T(8,128)S(1)} %get-tuple-element.15.spare_valid, f32[48,16,128]{2,1,0:T(8,128)S(1)} %get-tuple-element.16.peaks, ...), custom_call_target="tpu_custom_call" | custom-call | tf_op jit(solution)/shard_map/arrive/pallas_call | solution.py:544
  26.5 18.6 %all_to_all.25.recv = bf16[32,2,16,128]{3,2,1,0:T(8,128)(2,1)S(1)} all-to-all(bf16[32,2,16,128]{3,2,1,0:T(8,128)(2,1)S(1)} %arrive.1), channel_id=1, replica_groups=mesh['grp'=4,'dev'=32] {'dev'}, dimensions={0} | all-to-all | bytes 524288 | tf_op jit(solution)/shard_map/all_to_all | solution.py:556
  45.1 3.1 %project.1 = bf16[32,2,16,128]{3,2,1,0:T(8,128)(2,1)} custom-call(bf16[32,2,16,128]{3,2,1,0:T(8,128)(2,1)S(1)} %all_to_all.25.recv, bf16[192,6144]{1,0:T(8,128)(2,1)} %weight.1), custom_call_target="tpu_custom_call" | custom-call | tf_op jit(solution)/shard_map/project/pallas_call | solution.py:577
  48.3 3.8 %all-to-all-start.2 = ((bf16[32,2,16,128]{3,2,1,0:T(8,128)(2,1)}), bf16[32,2,16,128]{3,2,1,0:T(8,128)(2,1)S(1)}, u32[]{:S(2)}, u32[]{:S(2)}) async-start(bf16[32,2,16,128]{3,2,1,0:T(8,128)(2,1)} %project.1), calls=%async_computation.2 | async-start | bytes 524288 | tf_op jit(solution)/shard_map/all_to_all | solution.py:591
  52.1 0.1 copy.54
  52.1 0.1 copy.55
  52.2 0.1 eq.15
  52.3 0.2 convert_reduce_fusion
  52.5 0.1 reduce_sum.21
  52.6 0.1 copy.56
  52.7 0.1 pad_add_fusion.qrow
  52.8 8.2 %all-to-all-done.2.recv = bf16[32,2,16,128]{3,2,1,0:T(8,128)(2,1)S(1)} async-done(((bf16[32,2,16,128]{3,2,1,0:T(8,128)(2,1)}), bf16[32,2,16,128]{3,2,1,0:T(8,128)(2,1)S(1)}, u32[]{:S(2)}, u32[]{:S(2)}) %all-to-all-start.2) | async-done | bytes 262176 | tf_op jit(solution)/shard_map/all_to_all | solution.py:591
  60.9 0.3 dispatch.1
  61.2 17.1 %all_to_all.26.recv = bf16[128,16,128]{2,1,0:T(8,128)(2,1)S(1)} all-to-all(bf16[128,16,128]{2,1,0:T(8,128)(2,1)S(1)} %get-tuple-element.21), channel_id=1, replica_groups=mesh['grp'=4,'dev'=32] {'grp','dev'}, dimensions={0} | all-to-all | bytes 1048576 | tf_op jit(solution)/shard_map/all_to_all | solution.py:604
  78.3 8.3 %expert.1 = bf16[128,16,128]{2,1,0:T(8,128)(2,1)} custom-call(bf16[128,16,128]{2,1,0:T(8,128)(2,1)S(1)} %all_to_all.26.recv, bf16[6144,512]{1,0:T(8,128)(2,1)} %w_gate.1, bf16[6144,512]{1,0:T(8,128)(2,1)} %w_up.1, bf16[512,6144]{1,0:T(8,128)(2,1)} %w_down.1), custom_call_target="tpu_custom_call" | custom-call | tf_op jit(solution)/shard_map/expert/pallas_call | solution.py:607
  86.6 4.8 %all-to-all-start.4 = ((bf16[128,16,128]{2,1,0:T(8,128)(2,1)}), bf16[128,16,128]{2,1,0:T(8,128)(2,1)S(1)}, u32[]{:S(2)}, u32[]{:S(2)}) async-start(bf16[128,16,128]{2,1,0:T(8,128)(2,1)} %expert.1), calls=%async_computation.4 | async-start | bytes 1048576 | tf_op jit(solution)/shard_map/all_to_all | solution.py:624
  91.4 0.1 copy.58
  91.5 0.1 convert_reduce_fusion.1
  91.6 0.1 convert_divide_fusion.share
  91.7 4.0 %store.1 = (bf16[16,8,32,128]{3,2,1,0:T(8,128)(2,1)}, bf16[16,8,32,128]{3,2,1,0:T(8,128)(2,1)}) custom-call(s32[64]{0:T(128)} %source.5, s32[16]{0:T(128)} %lengths.3, bf16[16,8,32,128]{3,2,1,0:T(8,128)(2,1)} %cache_k.5, bf16[16,8,32,128]{3,2,1,0:T(8,128)(2,1)} %cache_v.5, bf16[4,2,2,8,32,128]{5,4,3,2,1,0:T(8,128)(2,1)S(1)} %all-to-all-done.moved, ...), custom_call_target="tpu_custom_call" | custom-call | bytes 8388608 | tf_op jit(solution)/shard_map/store/pallas_call | solution.py:558
  95.7 9.2 %all-to-all-done.4.recv = bf16[128,16,128]{2,1,0:T(8,128)(2,1)S(1)} async-done(((bf16[128,16,128]{2,1,0:T(8,128)(2,1)}), bf16[128,16,128]{2,1,0:T(8,128)(2,1)S(1)}, u32[]{:S(2)}, u32[]{:S(2)}) %all-to-all-start.4) | async-done | bytes 524320 | tf_op jit(solution)/shard_map/all_to_all | solution.py:624
  104.9 0.9 final.1
  (12 shorter events, 0.1 us)
Async XLA Ops:
  0.6 9.0 %copy-start = (bf16[16,6144]{1,0:T(8,128)(2,1)S(1)}, bf16[16,6144]{1,0:T(8,128)(2,1)}, u32[]{:S(2)}) copy-start(bf16[16,6144]{1,0:T(8,128)(2,1)} %param.19) | copy-start | bytes 589828
  3.7 48.3 %copy-start.5 = (s32[16,2]{0,1:T(2,128)S(1)}, s32[16,2]{0,1:T(2,128)}, u32[]{:S(2)}) copy-start(s32[16,2]{0,1:T(2,128)} %param.28) | copy-start | bytes 388
  3.8 19.3 %all-to-all-start = ((bf16[4,2,2,8,32,128]{5,4,3,2,1,0:T(8,128)(2,1)}), bf16[4,2,2,8,32,128]{5,4,3,2,1,0:T(8,128)(2,1)S(1)}, u32[]{:S(2)}, u32[]{:S(2)}) async-start(bf16[4,2,2,8,32,128]{5,4,3,2,1,0:T(8,128)(2,1)} %pack.1), calls=%async_computation | async-start | bytes 2097152 | tf_op jit(solution)/shard_map/all_to_all | solution.py:503
  9.7 0.7 copy-start.3
  10.4 0.7 copy-start.4
  48.3 12.7 %all-to-all-start.2 = ((bf16[32,2,16,128]{3,2,1,0:T(8,128)(2,1)}), bf16[32,2,16,128]{3,2,1,0:T(8,128)(2,1)S(1)}, u32[]{:S(2)}, u32[]{:S(2)}) async-start(bf16[32,2,16,128]{3,2,1,0:T(8,128)(2,1)} %project.1), calls=%async_computation.2 | async-start | bytes 524288 | tf_op jit(solution)/shard_map/all_to_all | solution.py:591
  78.3 13.1 %copy-start.6 = (s32[16,2]{0,1:T(2,128)S(1)}, s32[16,2]{0,1:T(2,128)}, u32[]{:S(2)}) copy-start(s32[16,2]{0,1:T(2,128)} %param.29) | copy-start | bytes 388
  78.3 13.4 %copy-start.1 = (bf16[16,8,128]{2,1,0:T(8,128)(2,1)S(1)}, bf16[16,8,128]{2,1,0:T(8,128)(2,1)}, u32[]{:S(2)}) copy-start(bf16[16,8,128]{2,1,0:T(8,128)(2,1)} %new_key.1) | copy-start | bytes 98308
  78.3 13.4 %copy-start.2 = (bf16[16,8,128]{2,1,0:T(8,128)(2,1)S(1)}, bf16[16,8,128]{2,1,0:T(8,128)(2,1)}, u32[]{:S(2)}) copy-start(bf16[16,8,128]{2,1,0:T(8,128)(2,1)} %new_value.1) | copy-start | bytes 98308
  86.6 18.3 %all-to-all-start.4 = ((bf16[128,16,128]{2,1,0:T(8,128)(2,1)}), bf16[128,16,128]{2,1,0:T(8,128)(2,1)S(1)}, u32[]{:S(2)}, u32[]{:S(2)}) async-start(bf16[128,16,128]{2,1,0:T(8,128)(2,1)} %expert.1), calls=%async_computation.4 | async-start | bytes 1048576 | tf_op jit(solution)/shard_map/all_to_all | solution.py:624

commit v3 on v2

--- a/solution.py
+++ b/solution.py
@@ -38,34 +38,38 @@
     return value >> bits, value & (size - 1)
 
 
-def pack_kernel(groups, per, source, cache_k, cache_v, out, src, buf, src_sem, in_sem, out_sem):
-    pltpu.make_async_copy(source, src, src_sem).start()
+def pack_kernel(groups, per, source, cache_k, cache_v, out, src, kbuf, vbuf, in_sem, out_sem):
+    loads = [
+        pltpu.make_async_copy(a, b, in_sem.at[j])
+        for j, (a, b) in enumerate(((source, src), (cache_k, kbuf), (cache_v, vbuf)))
+    ]
+    for copy in loads:
+        copy.start()
     me = lax.axis_index("grp")
-    pltpu.make_async_copy(source, src, src_sem).wait()
-    loads, stores = [], []
+    loads[0].wait()
+    picks = []
     for dest in range(groups):
         count = jnp.int32(0)
-        picks = [jnp.int32(0)] * MOVE
+        chosen = [jnp.int32(0)] * MOVE
         for slot in range(per):
             owner, old = places(src[dest * per + slot], per)
             mine = (owner == me) & (me != dest)
             for rank in range(MOVE):
-                picks[rank] = jnp.where(mine & (count == rank), old, picks[rank])
+                chosen[rank] = jnp.where(mine & (count == rank), old, chosen[rank])
             count = count + mine.astype(jnp.int32)
-        for rank in range(MOVE):
-            for which, cache in ((0, cache_k), (1, cache_v)):
+        picks.append(chosen)
+    stores = []
+    for which, buf in ((0, kbuf), (1, vbuf)):
+        loads[1 + which].wait()
+        for dest in range(groups):
+            for rank in range(MOVE):
                 copy = pltpu.make_async_copy(
-                    cache.at[picks[rank]], buf.at[dest, which, rank], in_sem.at[dest, which, rank]
+                    buf.at[picks[dest][rank]],
+                    out.at[dest, which, rank],
+                    out_sem.at[dest, which, rank],
                 )
                 copy.start()
-                loads.append((copy, dest, which, rank))
-    for load, dest, which, rank in loads:
-        load.wait()
-        copy = pltpu.make_async_copy(
-            buf.at[dest, which, rank], out.at[dest, which, rank], out_sem.at[dest, which, rank]
-        )
-        copy.start()
-        stores.append(copy)
+                stores.append(copy)
     for copy in stores:
         copy.wait()
 
@@ -79,9 +83,11 @@
 
 
 def stay_kernel(
-    groups, per, source, lengths, cache_k, cache_v, query, new_key, new_value, resid, gain,
-    spare_valid, peaks, totals, contexts, start, gains, kbuf, vbuf, src, length, sems,
+    groups, per, source, lengths, cache_k, cache_v, query, new_key, new_value, resid, gain, *refs
 ):
+    (
+    _, _, _, spare_valid, peaks, totals, contexts, start, gains, kbuf, vbuf, src, length, sems,
+    ) = refs
     copies = [
         pltpu.make_async_copy(a, b, sems.at[j])
         for j, (a, b) in enumerate(
@@ -154,7 +160,7 @@
         gains[k : k + 1] = jnp.where(spare[k], F32(0.0), jnp.sum(own, axis=0, keepdims=True))
 
 
-def arrive_kernel(moved, query, spare_valid, peaks, totals, contexts, out, buf, sems):
+def arrive_kernel(moved, query, spare_valid, peaks, totals, contexts, out):
     groups, _, _, heads_kv, block, _ = moved.shape
     share, per = query.shape[0] // heads_kv, query.shape[1]
     columns = groups * MOVE * block
@@ -165,7 +171,6 @@
     lane2 = iota((per, LANES), 1)
     first = ((lane2 >> 3) & 1) == 0
     low = lane2 < HALF
-    copies = []
     for kv in range(heads_kv):
         keys = moved[:, 0, :, kv].reshape(columns, LANES)
         values = moved[:, 1, :, kv].reshape(columns, LANES)
@@ -194,16 +199,10 @@
             m = kv * (share // 3) + i
             a, b, c = (context[3 * i + j] for j in range(3))
             sa, sb, sc = (stat[3 * i + j] for j in range(3))
-            buf[2 * m, 0] = a.astype(BF16)
-            buf[2 * m, 1] = jnp.where(low, b, jnp.where(first, sa, sb)).astype(BF16)
-            buf[2 * m + 1, 0] = jnp.where(low, jnp.where(first, sb, sc), b).astype(BF16)
-            buf[2 * m + 1, 1] = c.astype(BF16)
-        part = pl.ds(2 * kv * (share // 3), 2 * (share // 3))
-        copy = pltpu.make_async_copy(buf.at[part], out.at[part], sems.at[kv])
-        copy.start()
-        copies.append(copy)
-    for copy in copies:
-        copy.wait()
+            out[2 * m, 0] = a.astype(BF16)
+            out[2 * m, 1] = jnp.where(low, b, jnp.where(first, sa, sb)).astype(BF16)
+            out[2 * m + 1, 0] = jnp.where(low, jnp.where(first, sb, sc), b).astype(BF16)
+            out[2 * m + 1, 1] = c.astype(BF16)
 
 
 def store_kernel(
@@ -262,7 +261,7 @@
         copy.wait()
 
 
-def project_kernel(recv, weight, out, wbuf, buf, w_sems, sems):
+def project_kernel(recv, weight, out, wbuf, w_sems):
     span = wbuf.shape[2]
     loads = []
     for j in range(wbuf.shape[0]):
@@ -292,7 +291,6 @@
     both = jnp.concatenate(parts, axis=1)
     rows = weight.shape[0]
     attn = jnp.where(even, both[:, :rows], both[:, 2 * LANES - rows :]).astype(BF16)
-    copies = []
     for m in range(out.shape[0] // 2):
         j, at = divmod(3 * LANES * m, span)
         if at == 0:
@@ -301,16 +299,10 @@
             attn, wbuf[j, :, at : at + 3 * LANES], preferred_element_type=F32
         ).astype(BF16)
         t0, t1, t2 = (part[:, LANES * j : LANES * (j + 1)] for j in range(3))
-        buf[2 * m, 0] = t0
-        buf[2 * m, 1] = t1
-        buf[2 * m + 1, 0] = t1
-        buf[2 * m + 1, 1] = t2
-        part = pl.ds(2 * m, 2)
-        copy = pltpu.make_async_copy(buf.at[part], out.at[part], sems.at[m])
-        copy.start()
-        copies.append(copy)
-    for copy in copies:
-        copy.wait()
+        out[2 * m, 0] = t0
+        out[2 * m, 1] = t1
+        out[2 * m + 1, 0] = t1
+        out[2 * m + 1, 1] = t2
 
 
 def tiles_of(even, wide):
@@ -493,9 +485,9 @@
         out_specs=HBM,
         scratch_shapes=[
             pltpu.SMEM(source.shape, jnp.int32),
-            pltpu.VMEM(move_shape, BF16),
-            pltpu.SemaphoreType.DMA,
-            pltpu.SemaphoreType.DMA((groups, 2, MOVE)),
+            pltpu.VMEM(cache_k.shape, BF16),
+            pltpu.VMEM(cache_v.shape, BF16),
+            pltpu.SemaphoreType.DMA((3,)),
             pltpu.SemaphoreType.DMA((groups, 2, MOVE)),
         ],
         compiler_params=params(56 << 20),
@@ -524,7 +516,7 @@
             sds((2, per, LANES), F32),
             sds((2, LANES), F32),
         ),
-        in_specs=[HBM, HBM, HBM, HBM, VMEM, VMEM, VMEM, VMEM, VMEM],
+        in_specs=[HBM] * 4 + [VMEM] * 8,
         out_specs=(VMEM,) * 6,
         scratch_shapes=[
             pltpu.VMEM(cache_k.shape, BF16),
@@ -538,7 +530,7 @@
     )(
         source, lengths, cache_k, cache_v, by_head,
         new_key.transpose(1, 0, 2), new_value.transpose(1, 0, 2), resid,
-        norm_gain.reshape(-1, LANES),
+        norm_gain.reshape(-1, LANES), qrow, qcol, share,
     )
 
     ctx = pl.pallas_call(
@@ -546,11 +538,7 @@
         name="arrive",
         out_shape=sds((devs, 2, per, LANES), BF16),
         in_specs=[VMEM] * 6,
-        out_specs=HBM,
-        scratch_shapes=[
-            pltpu.VMEM((devs, 2, per, LANES), BF16),
-            pltpu.SemaphoreType.DMA((kv_heads,)),
-        ],
+        out_specs=VMEM,
         compiler_params=params(52 << 20),
     )(moved, by_head, spare_valid, peaks, totals, contexts)
     ctx = lax.all_to_all(ctx, "dev", split_axis=0, concat_axis=0, tiled=True)
@@ -579,12 +567,10 @@
         name="project",
         out_shape=sds((devs, 2, per, LANES), BF16),
         in_specs=[VMEM, HBM],
-        out_specs=HBM,
+        out_specs=VMEM,
         scratch_shapes=[
             pltpu.VMEM((8, out_weight.shape[0], width // 8), BF16),
-            pltpu.VMEM((devs, 2, per, LANES), BF16),
             pltpu.SemaphoreType.DMA((8,)),
-            pltpu.SemaphoreType.DMA((devs // 2,)),
         ],
         compiler_params=params(52 << 20),
     )(ctx, out_weight)

time: 107 us -> 102 us (0.953)
  blocking collectives: 35.7 us -> 48.1 us
  waiting for transfers between devices: 25.5 us -> 14.3 us
  starting transfers between devices: 13.6 us -> 9.62 us
  Pallas kernels: 27 us -> 23.3 us
  local copies, waits for them, and re-layouts: 2.74 us -> 4.09 us
    all_to_all x0 -> x1, blocking collectives: none -> 12.4 us  [on_device(): lax.all_to_all(partial_rows, 'dev', split_axis=0, concat_axis=0, tiled=True)]
    all_to_all x1 -> x0, waiting for transfers between devices: 8.18 us -> none  [on_device(): lax.all_to_all(partial_rows, 'dev', split_axis=0, concat_axis=0, tiled=True)]
    all_to_all x1 -> x0, starting transfers between devices: 3.77 us -> none  [on_device(): lax.all_to_all(partial_rows, 'dev', split_axis=0, concat_axis=0, tiled=True)]
    all_to_all x1, waiting for transfers between devices: 8.18 us -> 5.18 us  [on_device(): moved = lax.all_to_all(sent, 'grp', split_axis=0, concat_axis=0, tiled=True)]
    pallas_call x1, Pallas kernels: 3.45 us -> 0.73 us  [on_device(): pl.pallas_call(arrive_kernel, name='arrive', out_shape=sds((devs, 2, per,...]
    unnamed x16 -> x12, local copies, waits for them, and re-layouts: 1.59 us -> 2.92 us
  transfers between devices with their start and end apart: 3 -> 2, of which waited for: 3 -> 2; matrix products, arithmetic and copies ran while one was open for 2% -> 4% of each run, Pallas kernels for 7% -> 8%
where the time goes in v3:
time: 102 us; the launch traced here: 101 us
  blocking collectives  48.1 us (47%)
  Pallas kernels  23.3 us (23%)
  waiting for transfers between devices  14.3 us (14%)
  starting transfers between devices  9.62 us (9%)
  local copies, waits for them, and re-layouts  4.09 us (4%)
  other arithmetic  1.14 us (1%)
    all_to_all x1, blocking collectives, on_device(): ctx = lax.all_to_all(ctx, 'dev', split_axis=0, concat_axis=0, tiled=True)  18.6 us
    all_to_all x1, blocking collectives, on_device(): lax.all_to_all(rows, ('grp', 'dev'), split_axis=0, concat_axis=0, tiled=T...  17.1 us
    all_to_all x1, blocking collectives, on_device(): lax.all_to_all(partial_rows, 'dev', split_axis=0, concat_axis=0, tiled=True)  12.4 us
    all_to_all x1, waiting for transfers between devices, on_device(): lax.all_to_all(partial_out, ('grp', 'dev'), split_axis=0, concat_axis=0,...  9.1 us
    pallas_call x1, Pallas kernels, on_device(): pl.pallas_call(functools.partial(expert_kernel, groups), name='expert', o...  8.26 us
    all_to_all x1, waiting for transfers between devices, on_device(): moved = lax.all_to_all(sent, 'grp', split_axis=0, concat_axis=0, tiled=True)  5.18 us
    all_to_all x1, starting transfers between devices, on_device(): moved = lax.all_to_all(sent, 'grp', split_axis=0, concat_axis=0, tiled=True)  4.84 us
    all_to_all x1, starting transfers between devices, on_device(): lax.all_to_all(partial_out, ('grp', 'dev'), split_axis=0, concat_axis=0,...  4.78 us
  transfers between devices with their start and end apart: 2, of which 2 were waited for; matrix products, arithmetic and copies ran while one was open for 4% of the time, Pallas kernels for 8%

profile of v3, /device:TPU:1, one launch (start us, length us, event | category | flops | bytes accessed | tf_op | source)
XLA Modules:
  0.0 101.3 jit_solution(7718554296042216392)
XLA Ops:
  0.6 0.0 copy-start
  0.6 2.5 %pack.1 = bf16[4,2,2,8,32,128]{5,4,3,2,1,0:T(8,128)(2,1)} custom-call(s32[64]{0:T(128)} %source.5, bf16[16,8,32,128]{3,2,1,0:T(8,128)(2,1)} %cache_k.5, bf16[16,8,32,128]{3,2,1,0:T(8,128)(2,1)} %cache_v.5), custom_call_target="tpu_custom_call" | custom-call | tf_op jit(solution)/shard_map/pack/pallas_call | solution.py:480
  3.2 4.8 %all-to-all-start = ((bf16[4,2,2,8,32,128]{5,4,3,2,1,0:T(8,128)(2,1)}), bf16[4,2,2,8,32,128]{5,4,3,2,1,0:T(8,128)(2,1)S(1)}, u32[]{:S(2)}, u32[]{:S(2)}) async-start(bf16[4,2,2,8,32,128]{5,4,3,2,1,0:T(8,128)(2,1)} %pack.1), calls=%async_computation | async-start | bytes 2097152 | tf_op jit(solution)/shard_map/all_to_all | solution.py:495
  8.0 0.7 broadcast_multiply_fusion
  8.7 0.8 copy.56
  9.5 0.1 copy.57
  9.5 0.8 copy.60
  10.3 0.1 convert_reduce_fusion.1
  10.4 0.1 eq.15
  10.5 0.2 convert_reduce_fusion
  10.7 0.1 reduce_sum.21
  10.8 0.1 copy.58
  10.9 0.1 pad_add_fusion.refs_0_.qrow
  10.9 0.1 convert_divide_fusion.refs_2_.share
  11.0 0.8 copy_bitcast_fusion
  11.8 0.0 copy-done
  11.9 0.0 copy-start.3
  11.9 0.7 copy-done.3
  12.6 0.7 copy-done.4
  13.3 3.8 %stay.1 = (f32[16,256]{1,0:T(8,128)S(1)}, f32[48,16,128]{2,1,0:T(8,128)S(1)}, f32[48,16,128]{2,1,0:T(8,128)S(1)}, f32[48,16,128]{2,1,0:T(8,128)S(1)}, f32[2,16,128]{2,1,0:T(8,128)S(1)}, /*index=5*/f32[2,128]{1,0:T(2,128)S(1)}) custom-call(s32[64]{0:T(128)} %source.5, s32[16]{0:T(128)} %lengths.3, bf16[16,8,32,128]{3,2,1,0:T(8,128)(2,1)} %cache_k.5, ...), custom_call_target="tpu_custom_call" | custom-call | bytes 16777216 | tf_op jit(solution)/shard_map/stay/pallas_call | solution.py:508
  17.1 5.2 %all-to-all-done.moved = bf16[4,2,2,8,32,128]{5,4,3,2,1,0:T(8,128)(2,1)S(1)} async-done(((bf16[4,2,2,8,32,128]{5,4,3,2,1,0:T(8,128)(2,1)}), bf16[4,2,2,8,32,128]{5,4,3,2,1,0:T(8,128)(2,1)S(1)}, u32[]{:S(2)}, u32[]{:S(2)}) %all-to-all-start) | async-done | bytes 1048608 | tf_op jit(solution)/shard_map/all_to_all | solution.py:495
  22.3 0.7 arrive.1
  23.0 18.6 %all_to_all.25.recv = bf16[32,2,16,128]{3,2,1,0:T(8,128)(2,1)S(1)} all-to-all(bf16[32,2,16,128]{3,2,1,0:T(8,128)(2,1)S(1)} %arrive.1), channel_id=1, replica_groups=mesh['grp'=4,'dev'=32] {'dev'}, dimensions={0} | all-to-all | bytes 524288 | tf_op jit(solution)/shard_map/all_to_all | solution.py:544
  41.6 2.4 %project.1 = bf16[32,2,16,128]{3,2,1,0:T(8,128)(2,1)S(1)} custom-call(bf16[32,2,16,128]{3,2,1,0:T(8,128)(2,1)S(1)} %all_to_all.25.recv, bf16[192,6144]{1,0:T(8,128)(2,1)} %weight.1), custom_call_target="tpu_custom_call" | custom-call | tf_op jit(solution)/shard_map/project/pallas_call | solution.py:565
  44.0 12.4 %all_to_all.26.recv = bf16[32,2,16,128]{3,2,1,0:T(8,128)(2,1)S(1)} all-to-all(bf16[32,2,16,128]{3,2,1,0:T(8,128)(2,1)S(1)} %project.1), channel_id=1, replica_groups=mesh['grp'=4,'dev'=32] {'dev'}, dimensions={0} | all-to-all | bytes 524288 | tf_op jit(solution)/shard_map/all_to_all | solution.py:577
  56.4 0.3 dispatch.1
  56.7 17.1 %all_to_all.27.recv = bf16[128,16,128]{2,1,0:T(8,128)(2,1)S(1)} all-to-all(bf16[128,16,128]{2,1,0:T(8,128)(2,1)S(1)} %get-tuple-element.21), channel_id=1, replica_groups=mesh['grp'=4,'dev'=32] {'grp','dev'}, dimensions={0} | all-to-all | bytes 1048576 | tf_op jit(solution)/shard_map/all_to_all | solution.py:590
  73.8 8.3 %expert.1 = bf16[128,16,128]{2,1,0:T(8,128)(2,1)} custom-call(bf16[128,16,128]{2,1,0:T(8,128)(2,1)S(1)} %all_to_all.27.recv, bf16[6144,512]{1,0:T(8,128)(2,1)} %w_gate.1, bf16[6144,512]{1,0:T(8,128)(2,1)} %w_up.1, bf16[512,6144]{1,0:T(8,128)(2,1)} %w_down.1), custom_call_target="tpu_custom_call" | custom-call | tf_op jit(solution)/shard_map/expert/pallas_call | solution.py:593
  82.1 4.8 %all-to-all-start.4 = ((bf16[128,16,128]{2,1,0:T(8,128)(2,1)}), bf16[128,16,128]{2,1,0:T(8,128)(2,1)S(1)}, u32[]{:S(2)}, u32[]{:S(2)}) async-start(bf16[128,16,128]{2,1,0:T(8,128)(2,1)} %expert.1), calls=%async_computation.4 | async-start | bytes 1048576 | tf_op jit(solution)/shard_map/all_to_all | solution.py:610
  86.9 4.4 %store.1 = (bf16[16,8,32,128]{3,2,1,0:T(8,128)(2,1)}, bf16[16,8,32,128]{3,2,1,0:T(8,128)(2,1)}) custom-call(s32[64]{0:T(128)} %source.5, s32[16]{0:T(128)} %lengths.3, bf16[16,8,32,128]{3,2,1,0:T(8,128)(2,1)} %cache_k.5, bf16[16,8,32,128]{3,2,1,0:T(8,128)(2,1)} %cache_v.5, bf16[4,2,2,8,32,128]{5,4,3,2,1,0:T(8,128)(2,1)S(1)} %all-to-all-done.moved, ...), custom_call_target="tpu_custom_call" | custom-call | bytes 8388608 | tf_op jit(solution)/shard_map/store/pallas_call | solution.py:546
  91.2 9.1 %all-to-all-done.4.recv = bf16[128,16,128]{2,1,0:T(8,128)(2,1)S(1)} async-done(((bf16[128,16,128]{2,1,0:T(8,128)(2,1)}), bf16[128,16,128]{2,1,0:T(8,128)(2,1)S(1)}, u32[]{:S(2)}, u32[]{:S(2)}) %all-to-all-start.4) | async-done | bytes 524320 | tf_op jit(solution)/shard_map/all_to_all | solution.py:610
  100.3 0.9 final.1
  (7 shorter events, 0.1 us)
Async XLA Ops:
  0.6 11.2 %copy-start = (bf16[16,6144]{1,0:T(8,128)(2,1)S(1)}, bf16[16,6144]{1,0:T(8,128)(2,1)}, u32[]{:S(2)}) copy-start(bf16[16,6144]{1,0:T(8,128)(2,1)} %param.19) | copy-start | bytes 589828
  3.2 19.1 %all-to-all-start = ((bf16[4,2,2,8,32,128]{5,4,3,2,1,0:T(8,128)(2,1)}), bf16[4,2,2,8,32,128]{5,4,3,2,1,0:T(8,128)(2,1)S(1)}, u32[]{:S(2)}, u32[]{:S(2)}) async-start(bf16[4,2,2,8,32,128]{5,4,3,2,1,0:T(8,128)(2,1)} %pack.1), calls=%async_computation | async-start | bytes 2097152 | tf_op jit(solution)/shard_map/all_to_all | solution.py:495
  11.9 0.7 copy-start.3
  12.6 0.7 copy-start.4
  73.8 13.1 %copy-start.1 = (bf16[16,8,128]{2,1,0:T(8,128)(2,1)S(1)}, bf16[16,8,128]{2,1,0:T(8,128)(2,1)}, u32[]{:S(2)}) copy-start(bf16[16,8,128]{2,1,0:T(8,128)(2,1)} %new_key.1) | copy-start | bytes 98308
  73.8 13.1 %copy-start.2 = (bf16[16,8,128]{2,1,0:T(8,128)(2,1)S(1)}, bf16[16,8,128]{2,1,0:T(8,128)(2,1)}, u32[]{:S(2)}) copy-start(bf16[16,8,128]{2,1,0:T(8,128)(2,1)} %new_value.1) | copy-start | bytes 98308
  82.1 18.3 %all-to-all-start.4 = ((bf16[128,16,128]{2,1,0:T(8,128)(2,1)}), bf16[128,16,128]{2,1,0:T(8,128)(2,1)S(1)}, u32[]{:S(2)}, u32[]{:S(2)}) async-start(bf16[128,16,128]{2,1,0:T(8,128)(2,1)} %expert.1), calls=%async_computation.4 | async-start | bytes 1048576 | tf_op jit(solution)/shard_map/all_to_all | solution.py:610

commit v4 on v3

--- a/solution.py
+++ b/solution.py
@@ -12,6 +12,7 @@
 CAP = 8
 LANES = 128
 HALF = 64
+ORDER = (1, 0, 3, 2)
 F32 = jnp.float32
 BF16 = jnp.bfloat16
 VMEM = pl.BlockSpec(memory_space=pltpu.VMEM)
@@ -38,7 +39,18 @@
     return value >> bits, value & (size - 1)
 
 
-def pack_kernel(groups, per, source, cache_k, cache_v, out, src, kbuf, vbuf, in_sem, out_sem):
+def sendings(groups):
+    plan = []
+    for step in range(1, groups):
+        if 1 < step < groups - 1:
+            plan += [(step, (rank,)) for rank in range(MOVE)]
+        else:
+            plan.append((step, tuple(range(MOVE))))
+    return plan
+
+
+def pack_kernel(groups, per, source, cache_k, cache_v, *refs):
+    outs, (src, kbuf, vbuf, in_sem, out_sem) = refs[:-5], refs[-5:]
     loads = [
         pltpu.make_async_copy(a, b, in_sem.at[j])
         for j, (a, b) in enumerate(((source, src), (cache_k, kbuf), (cache_v, vbuf)))
@@ -48,12 +60,13 @@
     me = lax.axis_index("grp")
     loads[0].wait()
     picks = []
-    for dest in range(groups):
+    for step in range(1, groups):
+        dest = lax.rem(me + step, groups)
         count = jnp.int32(0)
         chosen = [jnp.int32(0)] * MOVE
         for slot in range(per):
             owner, old = places(src[dest * per + slot], per)
-            mine = (owner == me) & (me != dest)
+            mine = owner == me
             for rank in range(MOVE):
                 chosen[rank] = jnp.where(mine & (count == rank), old, chosen[rank])
             count = count + mine.astype(jnp.int32)
@@ -61,12 +74,10 @@
     stores = []
     for which, buf in ((0, kbuf), (1, vbuf)):
         loads[1 + which].wait()
-        for dest in range(groups):
-            for rank in range(MOVE):
+        for at, (out, (step, ranks)) in enumerate(zip(outs, sendings(groups))):
+            for j, rank in enumerate(ranks):
                 copy = pltpu.make_async_copy(
-                    buf.at[picks[dest][rank]],
-                    out.at[dest, which, rank],
-                    out_sem.at[dest, which, rank],
+                    buf.at[picks[step - 1][rank]], out.at[which, j], out_sem.at[at, which, j]
                 )
                 copy.start()
                 stores.append(copy)
@@ -86,12 +97,16 @@
     groups, per, source, lengths, cache_k, cache_v, query, new_key, new_value, resid, gain, *refs
 ):
     (
-    _, _, _, spare_valid, peaks, totals, contexts, start, gains, kbuf, vbuf, src, length, sems,
+        _, spare_valid, peaks, totals, contexts, start, gains,
+        kbuf, vbuf, src, length, nk, nv, own_resid, gain_all, sems,
     ) = refs
     copies = [
         pltpu.make_async_copy(a, b, sems.at[j])
         for j, (a, b) in enumerate(
-            ((source, src), (lengths, length), (cache_k, kbuf), (cache_v, vbuf))
+            (
+                (source, src), (lengths, length), (cache_k, kbuf), (cache_v, vbuf),
+                (new_key, nk), (new_value, nv), (resid, own_resid), (gain, gain_all),
+            )
         )
     ]
     for copy in copies:
@@ -114,15 +129,17 @@
         spot = length[slot] - base
         spots.append(spot)
         limits.append(jnp.where(owner == me, spot, -1))
-        arrivals.append(jnp.where(owner == me, -1, owner * MOVE + rank))
+        ahead = lax.rem(me - owner + groups, groups)
+        arrivals.append(jnp.where(owner == me, -1, (ahead - 1) * MOVE + rank))
     spot, limit, arrival = column(spots), column(limits), column(arrivals)
     which, where = places(iota((per, per * block), 1), block)
     valid = (which == iota((per, per * block), 0)) & (where < limit)
     which, where = places(iota((per, groups * MOVE * block), 1), block)
     spare_valid[...] = ((which == arrival) & (where < spot)).astype(F32)
     fresh = (spot >= 0) & (spot < block)
-    copies[2].wait()
-    copies[3].wait()
+    for copy in copies[2:]:
+        copy.wait()
+    new_keys, new_values = nk[...].astype(F32), nv[...].astype(F32)
     scale = LANES**-0.5
     for kv in range(heads_kv):
         keys = kbuf[:, kv].reshape(per * block, LANES)
@@ -134,7 +151,7 @@
         ).reshape(share, per, per * block) * scale
         scores = jnp.where(valid[None], scores, F32(-1e30))
         newest = jnp.sum(
-            rows.astype(F32) * new_key[kv].astype(F32)[None], axis=-1, keepdims=True
+            rows.astype(F32) * new_keys[:, kv][None], axis=-1, keepdims=True
         ) * scale
         newest = jnp.where(fresh[None], newest, F32(-1e30))
         peak = jnp.maximum(jnp.max(scores, axis=-1, keepdims=True), newest)
@@ -143,27 +160,34 @@
         total = jnp.sum(weights.astype(F32), axis=-1, keepdims=True) + added
         context = jnp.dot(
             weights.reshape(share * per, per * block), values, preferred_element_type=F32
-        ).reshape(share, per, LANES) + added * new_value[kv].astype(F32)[None]
+        ).reshape(share, per, LANES) + added * new_values[:, kv][None]
         at = slice(kv * share, (kv + 1) * share)
         peaks[at] = jnp.broadcast_to(peak, (share, per, LANES))
         totals[at] = jnp.broadcast_to(total, (share, per, LANES))
         contexts[at] = context
     dev = lax.axis_index("dev")
     even = dev % 2 == 0
-    tiles = tiles_of(even, resid[...].astype(F32))
+    tiles = tiles_of(even, own_resid[...].astype(F32))
     lane = iota((1, LANES), 1)
     spare = (jnp.logical_not(even) & (lane < HALF), even & (lane >= HALF))
     for k in range(2):
         start[k] = tiles[k]
         at = 3 * (dev // 2) + dev % 2 + k
-        own = jnp.where(iota(gain.shape, 0) == at, gain[...].astype(F32), F32(0.0))
+        own = jnp.where(iota(gain.shape, 0) == at, gain_all[...].astype(F32), F32(0.0))
         gains[k : k + 1] = jnp.where(spare[k], F32(0.0), jnp.sum(own, axis=0, keepdims=True))
 
 
-def arrive_kernel(moved, query, spare_valid, peaks, totals, contexts, out):
-    groups, _, _, heads_kv, block, _ = moved.shape
+def arrive_kernel(query, spare_valid, peaks, totals, contexts, *refs):
+    moved, out = refs[:-1], refs[-1]
+    heads_kv, block = moved[0].shape[2:4]
     share, per = query.shape[0] // heads_kv, query.shape[1]
-    columns = groups * MOVE * block
+    columns = spare_valid.shape[1]
+
+    def gather(which, kv):
+        blocks = [m[which, j, kv] for m in moved for j in range(m.shape[1])]
+        spare = columns // block - len(blocks)
+        return jnp.concatenate(blocks + blocks[:spare], axis=0)
+
     valid = spare_valid[...] > 0.5
     scale = LANES**-0.5
     ones = jnp.ones((columns, LANES), BF16)
@@ -172,8 +196,7 @@
     first = ((lane2 >> 3) & 1) == 0
     low = lane2 < HALF
     for kv in range(heads_kv):
-        keys = moved[:, 0, :, kv].reshape(columns, LANES)
-        values = moved[:, 1, :, kv].reshape(columns, LANES)
+        keys, values = gather(0, kv), gather(1, kv)
         at = slice(kv * share, (kv + 1) * share)
         scores = lax.dot_general(
             query[at].reshape(share * per, LANES), keys, (((1,), (1,)), ((), ())),
@@ -206,9 +229,10 @@
 
 
 def store_kernel(
-    groups, per, source, lengths, cache_k, cache_v, moved, new_key, new_value,
-    out_k, out_v, kbuf, vbuf, src, length, small_sem, in_sem, out_sem,
+    groups, per, source, lengths, cache_k, cache_v, new_key, new_value, *refs
 ):
+    moved = refs[:-9]
+    out_k, out_v, kbuf, vbuf, src, length, small_sem, in_sem, out_sem = refs[-9:]
     small = [
         pltpu.make_async_copy(source, src, small_sem.at[0]),
         pltpu.make_async_copy(lengths, length, small_sem.at[1]),
@@ -236,10 +260,14 @@
             pltpu.make_async_copy(cache_k.at[slot], kbuf.at[slot], in_sem.at[0, slot]).start()
             pltpu.make_async_copy(cache_v.at[slot], vbuf.at[slot], in_sem.at[1, slot]).start()
 
-        @pl.when(jnp.logical_not(stays))
-        def _():
-            pltpu.make_async_copy(moved.at[owner, 0, rank], kbuf.at[slot], in_sem.at[0, slot]).start()
-            pltpu.make_async_copy(moved.at[owner, 1, rank], vbuf.at[slot], in_sem.at[1, slot]).start()
+        ahead = lax.rem(me - owner + groups, groups)
+        for piece, (step, ranks) in zip(moved, sendings(groups)):
+            for j, chosen in enumerate(ranks):
+
+                @pl.when((ahead == step) & (rank == chosen))
+                def _():
+                    pltpu.make_async_copy(piece.at[0, j], kbuf.at[slot], in_sem.at[0, slot]).start()
+                    pltpu.make_async_copy(piece.at[1, j], vbuf.at[slot], in_sem.at[1, slot]).start()
 
     outs = []
     for slot in range(per):
@@ -475,24 +503,26 @@
         pltpu.with_memory_space_constraint(a, pltpu.HBM)
         for a in (cache_k, cache_v, source, lengths, out_weight, w_gate, w_up, w_down)
     )
-    move_shape = (groups, 2, MOVE, kv_heads, block, head_dim)
-
+    plan = sendings(groups)
     sent = pl.pallas_call(
         functools.partial(pack_kernel, groups, per),
         name="pack",
-        out_shape=sds(move_shape, BF16),
+        out_shape=[sds((2, len(ranks), kv_heads, block, head_dim), BF16) for _, ranks in plan],
         in_specs=[HBM, HBM, HBM],
-        out_specs=HBM,
+        out_specs=[HBM] * len(plan),
         scratch_shapes=[
             pltpu.SMEM(source.shape, jnp.int32),
             pltpu.VMEM(cache_k.shape, BF16),
             pltpu.VMEM(cache_v.shape, BF16),
             pltpu.SemaphoreType.DMA((3,)),
-            pltpu.SemaphoreType.DMA((groups, 2, MOVE)),
+            pltpu.SemaphoreType.DMA((len(plan), 2, MOVE)),
         ],
         compiler_params=params(56 << 20),
     )(source, cache_k, cache_v)
-    moved = lax.all_to_all(sent, "grp", split_axis=0, concat_axis=0, tiled=True)
+    moved = [None] * len(plan)
+    for at in sorted(range(len(plan)), key=ORDER.index):
+        ring = [(g, (g + plan[at][0]) % groups) for g in range(groups)]
+        moved[at] = lax.ppermute(sent[at], "grp", ring)
 
     flat = expert_ids.reshape(-1)
     order = jnp.arange(flat.shape[0], dtype=jnp.int32)
@@ -516,38 +546,45 @@
             sds((2, per, LANES), F32),
             sds((2, LANES), F32),
         ),
-        in_specs=[HBM] * 4 + [VMEM] * 8,
+        in_specs=[HBM] * 4 + [VMEM] + [HBM] * 4 + [VMEM],
         out_specs=(VMEM,) * 6,
         scratch_shapes=[
             pltpu.VMEM(cache_k.shape, BF16),
             pltpu.VMEM(cache_v.shape, BF16),
             pltpu.SMEM(source.shape, jnp.int32),
             pltpu.SMEM(lengths.shape, jnp.int32),
-            pltpu.SemaphoreType.DMA((4,)),
+            pltpu.VMEM(new_key.shape, BF16),
+            pltpu.VMEM(new_value.shape, BF16),
+            pltpu.VMEM(resid.shape, BF16),
+            pltpu.VMEM((width // LANES, LANES), BF16),
+            pltpu.SemaphoreType.DMA((8,)),
         ],
         compiler_params=params(48 << 20),
         cost_estimate=pl.CostEstimate(flops=0, transcendentals=0, bytes_accessed=16 << 20),
     )(
         source, lengths, cache_k, cache_v, by_head,
-        new_key.transpose(1, 0, 2), new_value.transpose(1, 0, 2), resid,
-        norm_gain.reshape(-1, LANES), qrow, qcol, share,
+        *(
+            pltpu.with_memory_space_constraint(a, pltpu.HBM)
+            for a in (new_key, new_value, resid, norm_gain.reshape(-1, LANES))
+        ),
+        qrow,
     )
 
     ctx = pl.pallas_call(
         arrive_kernel,
         name="arrive",
         out_shape=sds((devs, 2, per, LANES), BF16),
-        in_specs=[VMEM] * 6,
+        in_specs=[VMEM] * (5 + len(moved)),
         out_specs=VMEM,
         compiler_params=params(52 << 20),
-    )(moved, by_head, spare_valid, peaks, totals, contexts)
+    )(by_head, spare_valid, peaks, totals, contexts, *moved)
     ctx = lax.all_to_all(ctx, "dev", split_axis=0, concat_axis=0, tiled=True)
 
     new_k, new_v = pl.pallas_call(
         functools.partial(store_kernel, groups, per),
         name="store",
         out_shape=(sds(cache_k.shape, BF16), sds(cache_v.shape, BF16)),
-        in_specs=[HBM, HBM, HBM, HBM, pl.BlockSpec(memory_space=pl.ANY), VMEM, VMEM],
+        in_specs=[HBM] * 4 + [VMEM] * 2 + [pl.BlockSpec(memory_space=pl.ANY)] * len(moved),
         out_specs=(HBM, HBM),
         scratch_shapes=[
             pltpu.VMEM(cache_k.shape, BF16),
@@ -560,7 +597,7 @@
         ],
         compiler_params=params(52 << 20),
         cost_estimate=pl.CostEstimate(flops=0, transcendentals=0, bytes_accessed=8 << 20),
-    )(source, lengths, cache_k, cache_v, moved, new_key, new_value)
+    )(source, lengths, cache_k, cache_v, new_key, new_value, *moved)
 
     partial_rows = pl.pallas_call(
         project_kernel,

time: 102 us -> 99.4 us (0.975)
  local copies, waits for them, and re-layouts: 4.09 us -> 1.22 us
  waiting for transfers between devices: 14.3 us -> 12.2 us
  starting transfers between devices: 9.62 us -> 11.2 us
    ppermute x0 -> x4, starting transfers between devices: none -> 6.41 us  [on_device(): moved[at] = lax.ppermute(sent[at], 'grp', ring)]
    all_to_all x1 -> x0, waiting for transfers between devices: 5.18 us -> none  [on_device(): moved = lax.all_to_all(sent, 'grp', split_axis=0, concat_axis=0, tiled=True)]
    all_to_all x1 -> x0, starting transfers between devices: 4.84 us -> none  [on_device(): moved = lax.all_to_all(sent, 'grp', split_axis=0, concat_axis=0, tiled=True)]
    ppermute x0 -> x4, waiting for transfers between devices: none -> 3.53 us  [on_device(): moved[at] = lax.ppermute(sent[at], 'grp', ring)]
    unnamed x12 -> x10, local copies, waits for them, and re-layouts: 2.92 us -> 0.86 us
    all_to_all x1, blocking collectives: 17.1 us -> 18.8 us  [on_device(): lax.all_to_all(rows, ('grp', 'dev'), split_axis=0, concat_axis=0, tiled=T...]
  transfers between devices with their start and end apart: 2 -> 5, of which waited for: 2 -> 2; matrix products, arithmetic and copies ran while one was open for 4% -> 2% of each run, Pallas kernels for 8% -> 8%
where the time goes in v4:
time: 99.4 us; the launch traced here: 98.9 us
  blocking collectives  49 us (49%)
  Pallas kernels  23.5 us (24%)
  waiting for transfers between devices  12.2 us (12%)
  starting transfers between devices  11.2 us (11%)
  local copies, waits for them, and re-layouts  1.22 us (1%)
  other arithmetic  1.15 us (1%)
    all_to_all x1, blocking collectives, on_device(): lax.all_to_all(rows, ('grp', 'dev'), split_axis=0, concat_axis=0, tiled=T...  18.8 us
    all_to_all x1, blocking collectives, on_device(): ctx = lax.all_to_all(ctx, 'dev', split_axis=0, concat_axis=0, tiled=True)  17.7 us
    all_to_all x1, blocking collectives, on_device(): lax.all_to_all(partial_rows, 'dev', split_axis=0, concat_axis=0, tiled=True)  12.4 us
    all_to_all x1, waiting for transfers between devices, on_device(): lax.all_to_all(partial_out, ('grp', 'dev'), split_axis=0, concat_axis=0,...  8.64 us
    pallas_call x1, Pallas kernels, on_device(): pl.pallas_call(functools.partial(expert_kernel, groups), name='expert', o...  8.29 us
    ppermute x4, starting transfers between devices, on_device(): moved[at] = lax.ppermute(sent[at], 'grp', ring)  6.41 us
    all_to_all x1, starting transfers between devices, on_device(): lax.all_to_all(partial_out, ('grp', 'dev'), split_axis=0, concat_axis=0,...  4.78 us
    pallas_call x1, Pallas kernels, on_device(): pl.pallas_call(functools.partial(store_kernel, groups, per), name='store'...  4.54 us
  transfers between devices with their start and end apart: 5, of which 2 were waited for; matrix products, arithmetic and copies ran while one was open for 2% of the time, Pallas kernels for 8%

profile of v4, /device:TPU:1, one launch (start us, length us, event | category | flops | bytes accessed | tf_op | source)
XLA Modules:
  0.0 98.9 jit_solution(2345550814269520714)
XLA Ops:
  0.6 0.0 copy-start
  0.6 2.4 %pack.1 = (bf16[2,2,8,32,128]{4,3,2,1,0:T(8,128)(2,1)S(1)}, bf16[2,1,8,32,128]{4,3,2,1,0:T(8,128)(2,1)S(1)}, bf16[2,1,8,32,128]{4,3,2,1,0:T(8,128)(2,1)S(1)}, bf16[2,2,8,32,128]{4,3,2,1,0:T(8,128)(2,1)S(1)}) custom-call(s32[64]{0:T(128)} %source.5, bf16[16,8,32,128]{3,2,1,0:T(8,128)(2,1)} %cache_k.5, bf16[16,8,32,128]{3,2,1,0:T(8,128)(2,1)} %cache_v.5), custom_call_target="tpu_custom_call" | custom-call | tf_op jit(solution)/shard_map/pack/pallas_call | solution.py:507
  3.1 3.6 %collective-permute-start.1 = (bf16[2,1,8,32,128]{4,3,2,1,0:T(8,128)(2,1)S(1)}, bf16[2,1,8,32,128]{4,3,2,1,0:T(8,128)(2,1)S(1)}, u32[]{:S(2)}, u32[]{:S(2)}) collective-permute-start(bf16[2,1,8,32,128]{4,3,2,1,0:T(8,128)(2,1)S(1)} %get-tuple-element.18), channel_id=1, source_target_pairs={{0,64},{32,96},{64,0},{96,32},{1,65},{33,97},{65,1},{97,33},{2,66}... | collective-permute-start | bytes 393224 | tf_op jit(solution)/shard_map/ppermute | solution.py:525
  6.7 0.1 collective-permute-start.2
  6.8 1.3 %collective-permute-start = (bf16[2,2,8,32,128]{4,3,2,1,0:T(8,128)(2,1)S(1)}, bf16[2,2,8,32,128]{4,3,2,1,0:T(8,128)(2,1)S(1)}, u32[]{:S(2)}, u32[]{:S(2)}) collective-permute-start(bf16[2,2,8,32,128]{4,3,2,1,0:T(8,128)(2,1)S(1)} %get-tuple-element.17), channel_id=1, source_target_pairs={{0,32},{32,64},{64,96},{96,0},{1,33},{33,65},{65,97},{97,1},{2,34}... | collective-permute-start | bytes 786440 | tf_op jit(solution)/shard_map/ppermute | solution.py:525
  8.2 1.3 %collective-permute-start.3 = (bf16[2,2,8,32,128]{4,3,2,1,0:T(8,128)(2,1)S(1)}, bf16[2,2,8,32,128]{4,3,2,1,0:T(8,128)(2,1)S(1)}, u32[]{:S(2)}, u32[]{:S(2)}) collective-permute-start(bf16[2,2,8,32,128]{4,3,2,1,0:T(8,128)(2,1)S(1)} %get-tuple-element.20), channel_id=1, source_target_pairs={{0,96},{32,0},{64,32},{96,64},{1,97},{33,1},{65,33},{97,65},{2,98}... | collective-permute-start | bytes 786440 | tf_op jit(solution)/shard_map/ppermute | solution.py:525
  9.5 0.7 broadcast_multiply_fusion
  10.2 0.8 copy.46
  11.0 0.1 eq.15
  11.1 0.2 convert_reduce_fusion
  11.3 0.1 copy.47
  11.3 0.1 reduce_sum.21
  11.4 0.1 copy.48
  11.5 0.1 pad_add_fusion.refs_0_.qrow
  11.6 3.9 %stay.1 = (f32[16,256]{1,0:T(8,128)S(1)}, f32[48,16,128]{2,1,0:T(8,128)S(1)}, f32[48,16,128]{2,1,0:T(8,128)S(1)}, f32[48,16,128]{2,1,0:T(8,128)S(1)}, f32[2,16,128]{2,1,0:T(8,128)S(1)}, /*index=5*/f32[2,128]{1,0:T(2,128)S(1)}) custom-call(s32[64]{0:T(128)} %source.5, s32[16]{0:T(128)} %lengths.3, bf16[16,8,32,128]{3,2,1,0:T(8,128)(2,1)} %cache_k.5, ...), custom_call_target="tpu_custom_call" | custom-call | bytes 16777216 | tf_op jit(solution)/shard_map/stay/pallas_call | solution.py:538
  15.5 0.0 collective-permute-done.1.refs_1_
  15.5 0.0 collective-permute-done.2.refs_2_
  15.5 3.5 %collective-permute-done.refs_0_ = bf16[2,2,8,32,128]{4,3,2,1,0:T(8,128)(2,1)S(1)} collective-permute-done((bf16[2,2,8,32,128]{4,3,2,1,0:T(8,128)(2,1)S(1)}, bf16[2,2,8,32,128]{4,3,2,1,0:T(8,128)(2,1)S(1)}, u32[]{:S(2)}, u32[]{:S(2)}) %collective-permute-start) | collective-permute-done | bytes 262176 | tf_op jit(solution)/shard_map/ppermute | solution.py:525
  19.0 0.8 arrive.1
  19.8 17.7 %all_to_all.20.recv = bf16[32,2,16,128]{3,2,1,0:T(8,128)(2,1)S(1)} all-to-all(bf16[32,2,16,128]{3,2,1,0:T(8,128)(2,1)S(1)} %arrive.1), channel_id=1, replica_groups=mesh['grp'=4,'dev'=32] {'dev'}, dimensions={0} | all-to-all | bytes 524288 | tf_op jit(solution)/shard_map/all_to_all | solution.py:581
  37.5 2.4 %project.1 = bf16[32,2,16,128]{3,2,1,0:T(8,128)(2,1)S(1)} custom-call(bf16[32,2,16,128]{3,2,1,0:T(8,128)(2,1)S(1)} %all_to_all.20.recv, bf16[192,6144]{1,0:T(8,128)(2,1)} %weight.1), custom_call_target="tpu_custom_call" | custom-call | tf_op jit(solution)/shard_map/project/pallas_call | solution.py:602
  39.9 12.4 %all_to_all.21.recv = bf16[32,2,16,128]{3,2,1,0:T(8,128)(2,1)S(1)} all-to-all(bf16[32,2,16,128]{3,2,1,0:T(8,128)(2,1)S(1)} %project.1), channel_id=1, replica_groups=mesh['grp'=4,'dev'=32] {'dev'}, dimensions={0} | all-to-all | bytes 524288 | tf_op jit(solution)/shard_map/all_to_all | solution.py:614
  52.3 0.3 dispatch.1
  52.6 18.8 %all_to_all.22.recv = bf16[128,16,128]{2,1,0:T(8,128)(2,1)S(1)} all-to-all(bf16[128,16,128]{2,1,0:T(8,128)(2,1)S(1)} %get-tuple-element.29), channel_id=1, replica_groups=mesh['grp'=4,'dev'=32] {'grp','dev'}, dimensions={0} | all-to-all | bytes 1048576 | tf_op jit(solution)/shard_map/all_to_all | solution.py:627
  71.4 8.3 %expert.1 = bf16[128,16,128]{2,1,0:T(8,128)(2,1)} custom-call(bf16[128,16,128]{2,1,0:T(8,128)(2,1)S(1)} %all_to_all.22.recv, bf16[6144,512]{1,0:T(8,128)(2,1)} %w_gate.1, bf16[6144,512]{1,0:T(8,128)(2,1)} %w_up.1, bf16[512,6144]{1,0:T(8,128)(2,1)} %w_down.1), custom_call_target="tpu_custom_call" | custom-call | tf_op jit(solution)/shard_map/expert/pallas_call | solution.py:630
  79.7 4.8 %all-to-all-start.3 = ((bf16[128,16,128]{2,1,0:T(8,128)(2,1)}), bf16[128,16,128]{2,1,0:T(8,128)(2,1)S(1)}, u32[]{:S(2)}, u32[]{:S(2)}) async-start(bf16[128,16,128]{2,1,0:T(8,128)(2,1)} %expert.1), calls=%async_computation.3 | async-start | bytes 1048576 | tf_op jit(solution)/shard_map/all_to_all | solution.py:647
  84.5 0.1 copy.50
  84.6 0.1 convert_reduce_fusion.1
  84.7 0.1 convert_divide_fusion.share
  84.8 4.5 %store.1 = (bf16[16,8,32,128]{3,2,1,0:T(8,128)(2,1)}, bf16[16,8,32,128]{3,2,1,0:T(8,128)(2,1)}) custom-call(s32[64]{0:T(128)} %source.5, s32[16]{0:T(128)} %lengths.3, bf16[16,8,32,128]{3,2,1,0:T(8,128)(2,1)} %cache_k.5, bf16[16,8,32,128]{3,2,1,0:T(8,128)(2,1)} %cache_v.5, bf16[16,8,128]{2,1,0:T(8,128)(2,1)S(1)} %copy-done.1, ...), custom_call_target="tpu_custom_call" | custom-call | bytes 8388608 | tf_op jit(solution)/shard_map/store/pallas_call | solution.py:583
  89.4 8.6 %all-to-all-done.3.recv = bf16[128,16,128]{2,1,0:T(8,128)(2,1)S(1)} async-done(((bf16[128,16,128]{2,1,0:T(8,128)(2,1)}), bf16[128,16,128]{2,1,0:T(8,128)(2,1)S(1)}, u32[]{:S(2)}, u32[]{:S(2)}) %all-to-all-start.3) | async-done | bytes 524320 | tf_op jit(solution)/shard_map/all_to_all | solution.py:647
  98.0 0.9 final.1
  (10 shorter events, 0.1 us)
Async XLA Ops:
  0.6 8.9 %copy-start = (bf16[16,6144]{1,0:T(8,128)(2,1)S(1)}, bf16[16,6144]{1,0:T(8,128)(2,1)}, u32[]{:S(2)}) copy-start(bf16[16,6144]{1,0:T(8,128)(2,1)} %param.19) | copy-start | bytes 589828
  3.1 12.4 %collective-permute-start.1 = (bf16[2,1,8,32,128]{4,3,2,1,0:T(8,128)(2,1)S(1)}, bf16[2,1,8,32,128]{4,3,2,1,0:T(8,128)(2,1)S(1)}, u32[]{:S(2)}, u32[]{:S(2)}) collective-permute-start(bf16[2,1,8,32,128]{4,3,2,1,0:T(8,128)(2,1)S(1)} %get-tuple-element.18), channel_id=1, source_target_pairs={{0,64},{32,96},{64,0},{96,32},{1,65},{33,97},{65,1},{97,33},{2,66}... | collective-permute-start | bytes 393224 | tf_op jit(solution)/shard_map/ppermute | solution.py:525
  6.7 8.7 %collective-permute-start.2 = (bf16[2,1,8,32,128]{4,3,2,1,0:T(8,128)(2,1)S(1)}, bf16[2,1,8,32,128]{4,3,2,1,0:T(8,128)(2,1)S(1)}, u32[]{:S(2)}, u32[]{:S(2)}) collective-permute-start(bf16[2,1,8,32,128]{4,3,2,1,0:T(8,128)(2,1)S(1)} %get-tuple-element.19), channel_id=1, source_target_pairs={{0,64},{32,96},{64,0},{96,32},{1,65},{33,97},{65,1},{97,33},{2,66}... | collective-permute-start | bytes 393224 | tf_op jit(solution)/shard_map/ppermute | solution.py:525
  6.8 12.2 %collective-permute-start = (bf16[2,2,8,32,128]{4,3,2,1,0:T(8,128)(2,1)S(1)}, bf16[2,2,8,32,128]{4,3,2,1,0:T(8,128)(2,1)S(1)}, u32[]{:S(2)}, u32[]{:S(2)}) collective-permute-start(bf16[2,2,8,32,128]{4,3,2,1,0:T(8,128)(2,1)S(1)} %get-tuple-element.17), channel_id=1, source_target_pairs={{0,32},{32,64},{64,96},{96,0},{1,33},{33,65},{65,97},{97,1},{2,34}... | collective-permute-start | bytes 786440 | tf_op jit(solution)/shard_map/ppermute | solution.py:525
  8.2 10.8 %collective-permute-start.3 = (bf16[2,2,8,32,128]{4,3,2,1,0:T(8,128)(2,1)S(1)}, bf16[2,2,8,32,128]{4,3,2,1,0:T(8,128)(2,1)S(1)}, u32[]{:S(2)}, u32[]{:S(2)}) collective-permute-start(bf16[2,2,8,32,128]{4,3,2,1,0:T(8,128)(2,1)S(1)} %get-tuple-element.20), channel_id=1, source_target_pairs={{0,96},{32,0},{64,32},{96,64},{1,97},{33,1},{65,33},{97,65},{2,98}... | collective-permute-start | bytes 786440 | tf_op jit(solution)/shard_map/ppermute | solution.py:525
  71.4 13.1 %copy-start.3 = (s32[16,2]{0,1:T(2,128)S(1)}, s32[16,2]{0,1:T(2,128)}, u32[]{:S(2)}) copy-start(s32[16,2]{0,1:T(2,128)} %param.29) | copy-start | bytes 388
  71.4 13.4 %copy-start.1 = (bf16[16,8,128]{2,1,0:T(8,128)(2,1)S(1)}, bf16[16,8,128]{2,1,0:T(8,128)(2,1)}, u32[]{:S(2)}) copy-start(bf16[16,8,128]{2,1,0:T(8,128)(2,1)} %new_key.3) | copy-start | bytes 98308
  71.4 13.4 %copy-start.2 = (bf16[16,8,128]{2,1,0:T(8,128)(2,1)S(1)}, bf16[16,8,128]{2,1,0:T(8,128)(2,1)}, u32[]{:S(2)}) copy-start(bf16[16,8,128]{2,1,0:T(8,128)(2,1)} %new_value.3) | copy-start | bytes 98308
  79.7 18.3 %all-to-all-start.3 = ((bf16[128,16,128]{2,1,0:T(8,128)(2,1)}), bf16[128,16,128]{2,1,0:T(8,128)(2,1)S(1)}, u32[]{:S(2)}, u32[]{:S(2)}) async-start(bf16[128,16,128]{2,1,0:T(8,128)(2,1)} %expert.1), calls=%async_computation.3 | async-start | bytes 1048576 | tf_op jit(solution)/shard_map/all_to_all | solution.py:647
